TPU v7x, 256 devices: a whole 4x4x8 slice. The times are simulated.
256 devices in a mesh: date: 8 (over y, core), tile: 32 (over x, z).
Axes of the slice: x: 4, y: 4, z: 8, core: 2. Of those that a mesh axis runs over, the one named last changes fastest.
Arguments:
- radar_echoes: bfloat16 [2048, 16, 32, 2, 256], P('tile', None, 'date')
- destination_panel: int32 [2048, 1], P('tile'), may hold values from 0 to 31; in each aligned block of 64 rows (0 to 63, 64 to 127, ...) at most 3 rows name the same one
- panel_line_shift: int32 [2048], P('tile'), may hold values from 0 to 240
- epoch_couples: int32 [64, 2], replicated, may hold values from 0 to 31, as said below
Outputs:
- coherence: float32 [8192, 64, 256], P('tile', 'date')
Inputs may be any that keep to these rules, and one draw needn't show every extreme that they name: `destination_panel`: of the blocks held by one index of tile, at most 3 land on the same tile; some index reaches it. `epoch_couples`: each row names an earlier date and a later one, 1 to 3 dates apart.
All inputs are finite; a program needn't handle non-finite values.
Results may differ from a plain program's by a relative error of at most 0.00079.
Values may be sent and summed in bfloat16 or wider, within the bound.
A program may use at most 64 MiB of HBM per device.

v0:
```python
import jax
import jax.numpy as jnp
from jax import lax
from jax.sharding import PartitionSpec as P

TR = 256


def window_sum(field, rows):
    total = field[0:rows]
    for row_lag in range(1, 7):
        total = total + field[row_lag : row_lag + rows]
    cols = total.shape[-1]
    padded = jnp.pad(total, ((0, 0), (0, 0), (7, 7)))
    result = padded[..., 0:cols]
    for column_lag in range(1, 15):
        result = result + padded[..., column_lag : column_lag + cols]
    return result


def coherence_of(first, second, rows):
    first = first.astype(jnp.float32)
    second = second.astype(jnp.float32)
    first_re, first_im = (first[:, :, 0], first[:, :, 1])
    second_re, second_im = (second[:, :, 0], second[:, :, 1])
    cross_re = first_re * second_re + first_im * second_im
    cross_im = first_im * second_re - first_re * second_im
    power_a = first_re * first_re + first_im * first_im
    power_e = second_re * second_re + second_im * second_im
    box_re = window_sum(cross_re, rows)
    box_im = window_sum(cross_im, rows)
    box_a = window_sum(power_a, rows)
    box_e = window_sum(power_e, rows)
    return jnp.sqrt(box_re * box_re + box_im * box_im) / jnp.sqrt(jnp.maximum(box_a * box_e, 1.0))


def local(radar_echoes, destination_panel, panel_line_shift, epoch_couples):
    patch_number = radar_echoes.shape[0]
    patch_height = radar_echoes.shape[1]
    epoch_here = radar_echoes.shape[2]
    panel_width = radar_echoes.shape[4]
    tile_count = lax.axis_size("tile")
    date_axis = lax.axis_size("date")
    capacity = max(2, patch_number // tile_count + max(1, patch_number // (2 * tile_count)))
    slot_count = tile_count * capacity
    target = destination_panel[:, 0]
    ordinal = jnp.arange(patch_number)
    earlier_same = (target[:, None] == target[None, :]) & (ordinal[None, :] < ordinal[:, None])
    rank_within = jnp.sum(earlier_same.astype(jnp.int32), axis=1)
    slot_of = target * capacity + rank_within
    chooser = jnp.arange(slot_count)[:, None] == slot_of[None, :]
    serial_patches = radar_echoes.reshape(patch_number, -1)
    send_blocks = jnp.dot(
        chooser.astype(jnp.bfloat16), serial_patches, preferred_element_type=jnp.float32
    )
    send_blocks = send_blocks.astype(jnp.bfloat16).reshape(
        slot_count, patch_height, epoch_here, 2, panel_width
    )
    send_offset = jnp.sum(jnp.where(chooser, panel_line_shift[None, :], 0), axis=1)
    got_blocks, got_offset = (
        lax.all_to_all(send_blocks, "tile", split_axis=0, concat_axis=0, tiled=True),
        lax.all_to_all(send_offset, "tile", split_axis=0, concat_axis=0, tiled=True),
    )
    tile_row = jnp.arange(TR)[:, None, None]
    inner_row = jnp.arange(patch_height)[None, None, :]
    placing = (tile_row == got_offset[None, :, None] + inner_row).astype(jnp.bfloat16)
    placing = placing.reshape(TR, slot_count * patch_height)
    panel_raster = jnp.dot(
        placing,
        got_blocks.reshape(slot_count * patch_height, -1),
        preferred_element_type=jnp.float32,
    )
    panel_raster = panel_raster.astype(jnp.bfloat16).reshape(TR, epoch_here, 2, panel_width)
    pair_local = epoch_couples.shape[0] // date_axis
    all_dates = lax.all_gather(panel_raster, "date", axis=1, tiled=True)
    mine = lax.dynamic_slice_in_dim(
        epoch_couples, lax.axis_index("date") * pair_local, pair_local, 0
    )
    padded = jnp.pad(all_dates, ((3, 3), (0, 0), (0, 0), (0, 0)))
    first = jnp.take(padded, mine[:, 0], axis=1)
    second = jnp.take(padded, mine[:, 1], axis=1)
    return coherence_of(first, second, TR)


def solution(mesh):
    in_specs = (P("tile", None, "date", None, None), P("tile", None), P("tile"), P())
    out_specs = P("tile", "date", None)
    return jax.shard_map(local, mesh=mesh, in_specs=in_specs, out_specs=out_specs, check_vma=False)
```

profile of v0, /device:TPU:1, one launch (start us, length us, event | category | flops | bytes accessed | tf_op | source)
XLA Modules:
  0.0 372.8 jit_solution(1310809890568040186)
XLA Ops:
  6.5 0.0 copy-start
  6.5 0.9 convert_reduce_fusion
  7.4 0.7 multiply_add_fusion.2
  8.1 0.8 select_reduce_fusion
  8.9 0.7 all_to_all.9
  9.6 11.9 %all-to-all-start = ((s32[32,3,1]{1,2,0:T(1,128)}), s32[32,3,1]{1,2,0:T(1,128)S(1)}, u32[]{:S(2)}, u32[]{:S(2)}) async-start(s32[32,3,1]{1,2,0:T(1,128)} %bitcast.2), calls=%async_computation | async-start | bytes 32768 | tf_op jit(solution)/shard_map/all_to_all | solution.py:62
  21.4 7.8 %reshape.107 = bf16[64,32768]{1,0:T(8,128)(2,1)} reshape(bf16[64,16,4,2,256]{4,3,2,1,0:T(2,128)(2,1)} %param.6) | data formatting | bytes 8388608 | tf_op jit(solution)/shard_map/reshape | solution.py:52
  29.2 6.7 %convolution_convert_fusion = bf16[96,32768]{1,0:T(8,128)(2,1)} fusion(bf16[64,32768]{1,0:T(8,128)(2,1)} %reshape.107, s32[64]{0:T(128)S(1)} %multiply_add_fusion.2), kind=kOutput, calls=%fused_computation.2 | convolution fusion | flops 405805056 | bytes 10486016 | tf_op jit(solution)/shard_map/dot_general | solution.py:53
  35.9 11.1 %reshape.108 = bf16[96,16,4,2,256]{4,3,2,1,0:T(2,128)(2,1)} reshape(bf16[96,32768]{1,0:T(8,128)(2,1)} %convolution_convert_fusion) | data formatting | bytes 12582912 | tf_op jit(solution)/shard_map/reshape | solution.py:56
  47.0 0.0 all-to-all-done
  47.0 9.3 %all-to-all-start.1 = ((bf16[96,16,4,2,256]{4,3,2,1,0:T(2,128)(2,1)}), bf16[96,16,4,2,256]{4,3,2,1,0:T(2,128)(2,1)}, u32[]{:S(2)}, u32[]{:S(2)}) async-start(bf16[96,16,4,2,256]{4,3,2,1,0:T(2,128)(2,1)} %reshape.108), calls=%async_computation.1 | async-start | bytes 12582912 | tf_op jit(solution)/shard_map/all_to_all | solution.py:61
  56.4 0.2 all-gather.2.cloned.1.call-start
  56.6 0.1 add.323
  56.7 0.5 broadcast.88
  57.2 0.7 reduce.3
  57.9 0.1 add.319
  58.0 0.1 add.320
  58.1 0.1 add.321
  58.2 138.1 %all-to-all-done.1 = bf16[96,16,4,2,256]{4,3,2,1,0:T(2,128)(2,1)} async-done(((bf16[96,16,4,2,256]{4,3,2,1,0:T(2,128)(2,1)}), bf16[96,16,4,2,256]{4,3,2,1,0:T(2,128)(2,1)}, u32[]{:S(2)}, u32[]{:S(2)}) %all-to-all-start.1) | async-done | bytes 6291488 | tf_op jit(solution)/shard_map/all_to_all | solution.py:61
  196.3 11.1 %reshape.109 = bf16[1536,2048]{1,0:T(8,128)(2,1)} reshape(bf16[96,16,4,2,256]{4,3,2,1,0:T(2,128)(2,1)} %all-to-all-done.1) | data formatting | bytes 12582912 | tf_op jit(solution)/shard_map/reshape | solution.py:70
  207.4 4.6 %convolution_convert_fusion.1 = bf16[256,2048]{1,0:T(8,128)(2,1)S(1)} fusion(bf16[1536,2048]{1,0:T(8,128)(2,1)} %reshape.109, s32[1536]{0:T(1024)S(1)} %add.324), kind=kOutput, calls=%fused_computation.59 | convolution fusion | flops 1611530240 | bytes 7346176 | tf_op jit(solution)/shard_map/dot_general | solution.py:68
  212.0 1.6 reshape.110
  213.6 0.0 all-gather.2.cloned.1.call-update
  213.6 0.0 copy-done
  213.6 0.1 constant_dynamic-slice_fusion
  213.8 56.9 %all-gather.2.cloned.1.call-done = bf16[256,32,2,256]{3,2,1,0:T(2,128)(2,1)} async-done(((bf16[256,4,2,256]{3,2,1,0:T(2,128)(2,1)}), bf16[256,32,2,256]{3,2,1,0:T(2,128)(2,1)}) %all-gather.2.cloned.1.call-update) | async-done | bytes 8388624 | tf_op jit(solution)/shard_map/all_gather | solution.py:75
  270.6 9.0 %pad.17 = bf16[262,32,2,256]{3,2,1,0:T(2,128)(2,1)} pad(bf16[256,32,2,256]{3,2,1,0:T(2,128)(2,1)} %all-gather.2.cloned.1.call-done, bf16[]{:T(256)} %constant.8.clone.1), padding=3_3x0_0x0_0x0_0 | pad | bytes 16973826 | tf_op jit(solution)/shard_map/jit(_pad)/pad | solution.py:79
  279.6 10.4 %gather_fusion.1 = bf16[8,262,2,256]{3,2,1,0:T(2,128)(2,1)S(1)} fusion(bf16[262,32,2,256]{3,2,1,0:T(2,128)(2,1)} %pad.17, s32[1024]{0:T(1024)S(1)} %pad_clamp_fusion), kind=kCustom, calls=%fused_computation.1.clone | custom fusion | bytes 4292640 | tf_op jit(solution)/shard_map/jit(_take)/gather | solution.py:81
  290.0 10.3 %gather_fusion = bf16[8,262,2,256]{3,2,1,0:T(2,128)(2,1)} fusion(bf16[262,32,2,256]{3,2,1,0:T(2,128)(2,1)} %pad.17, s32[1024]{0:T(1024)S(1)} %pad_clamp_fusion.1), kind=kCustom, calls=%fused_computation.clone | custom fusion | bytes 4292640 | tf_op jit(solution)/shard_map/jit(_take)/gather | solution.py:80
  300.3 2.5 bitcast_convert_fusion
  302.8 0.3 bitcast_add_fusion
  303.1 0.7 multiply_add_fusion.1
  303.7 0.4 fusion.60
  304.2 1.8 fusion.61
  305.9 1.7 fusion.62
  307.7 1.7 fusion.63
  309.4 0.0 copy-start.1
  309.4 56.5 %rsqrt_multiply_fusion = f32[256,8,256]{2,1,0:T(8,128)} fusion(f32[256,8,256]{2,1,0:T(8,128)S(1)} %fusion.60, f32[256,8,256]{2,1,0:T(8,128)} %fusion.61, f32[256,8,256]{2,1,0:T(8,128)} %fusion.62, f32[256,8,256]{2,1,0:T(8,128)} %fusion.63), kind=kLoop, calls=%fused_computation.157 | loop fusion | flops 32505856 | bytes 10485760 | tf_op jit(solution)/shard_map/div | solution.py:34
  366.0 0.0 copy-done.1
  (5 shorter events, 0.0 us)
Async XLA Ops:
  6.5 207.1 %copy-start = (s32[64,2]{0,1:T(2,128)S(1)}, s32[64,2]{0,1:T(2,128)}, u32[]{:S(2)}) copy-start(s32[64,2]{0,1:T(2,128)} %param.9) | copy-start | bytes 1540
  9.6 37.5 %all-to-all-start = ((s32[32,3,1]{1,2,0:T(1,128)}), s32[32,3,1]{1,2,0:T(1,128)S(1)}, u32[]{:S(2)}, u32[]{:S(2)}) async-start(s32[32,3,1]{1,2,0:T(1,128)} %bitcast.2), calls=%async_computation | async-start | bytes 32768 | tf_op jit(solution)/shard_map/all_to_all | solution.py:62
  47.0 149.3 %all-to-all-start.1 = ((bf16[96,16,4,2,256]{4,3,2,1,0:T(2,128)(2,1)}), bf16[96,16,4,2,256]{4,3,2,1,0:T(2,128)(2,1)}, u32[]{:S(2)}, u32[]{:S(2)}) async-start(bf16[96,16,4,2,256]{4,3,2,1,0:T(2,128)(2,1)} %reshape.108), calls=%async_computation.1 | async-start | bytes 12582912 | tf_op jit(solution)/shard_map/all_to_all | solution.py:61
  56.4 214.2 %all-gather.2.cloned.1.call-start = ((), (), s32[]{:S(2)}) async-start(), calls=%async_computation.2 | async-start | bytes 9437184 | tf_op jit(solution)/shard_map/all_gather | solution.py:75
  309.4 56.6 %copy-start.1 = (s32[64,2]{0,1:T(2,128)S(1)}, s32[64,2]{0,1:T(2,128)}, u32[]{:S(2)}) copy-start(s32[64,2]{0,1:T(2,128)} %param.9) | copy-start | bytes 1540
Sparse Core Ops, SparseCore 0:
  213.8 56.8 all-gather.1
where the time goes:
time: 374 us; the launch traced here: 373 us
  waiting for transfers between devices  195 us (52%)
  other arithmetic  68.7 us (18%)
  local copies, waits for them, and re-layouts  62.9 us (17%)
  starting transfers between devices  21.4 us (6%)
  between operations  13.5 us (4%)
  matrix products  11.3 us (3%)
    all_to_all x1, waiting for transfers between devices, local(): lax.all_to_all(send_blocks, 'tile', split_axis=0, concat_axis=0, tiled=True)  138 us
    all_gather x1, waiting for transfers between devices, local(): all_dates = lax.all_gather(panel_raster, 'date', axis=1, tiled=True)  56.9 us
    div x1, other arithmetic, coherence_of(): jnp.sqrt(box_re * box_re + box_im * box_im)  56.5 us
    all_to_all x1, starting transfers between devices, local(): lax.all_to_all(send_offset, 'tile', split_axis=0, concat_axis=0, tiled=True)  11.9 us
    reshape x1, local copies, waits for them, and re-layouts, local(): send_blocks.astype(jnp.bfloat16)  11.1 us
    reshape x1, local copies, waits for them, and re-layouts, local(): got_blocks.reshape(slot_count * patch_height, -1)  11.1 us
    gather x1, local copies, waits for them, and re-layouts, local(): second = jnp.take(padded, mine[:, 1], axis=1)  10.4 us
    gather x1, local copies, waits for them, and re-layouts, local(): first = jnp.take(padded, mine[:, 0], axis=1)  10.3 us
  transfers between devices with their start and end apart: 3, of which 2 were waited for; matrix products, arithmetic and copies ran while one was open for 7% of the time, Pallas kernels for 0%

commit v1 on v0

v1 whole, which is shorter than its diff:
```python
import functools

import jax
import jax.numpy as jnp
from jax import lax
from jax.experimental import pallas as pl
from jax.experimental.pallas import tpu as pltpu
from jax.sharding import PartitionSpec as P

NX, NZ, NY = 4, 8, 4
NT = NX * NZ
TR = 256
BR = 16
CAP = 3
BLK = 64
NQ = 8
KS = CAP * BR * 2
KP = 128
NP = 8
MSG = 2 * TR + 16
LEVELS = 32000.0
MESH = pl.DeviceIdType.MESH


def sort_kernel(dest, shift, x_ref, z_ref, koff_ref, held, zeros, count, block_of, in_sem, out_sem):
    loads = []
    for q in range(NQ):
        half, date = divmod(q, 4)
        copy = pltpu.make_async_copy(
            x_ref.at[:, :, date, :, pl.ds(half * 128, 128)], held.at[q], in_sem.at[q]
        )
        copy.start()
        loads.append(copy)
    zeros[...] = jnp.zeros_like(zeros)

    @pl.loop(0, NT)
    def _(t):
        count[t] = 0

    @pl.loop(0, NT * CAP)
    def _(s):
        block_of[s] = -1

    @pl.loop(0, BLK)
    def _(b):
        t = dest[b]
        k = count[t]
        count[t] = k + 1
        block_of[t * CAP + k] = b

    lane = lax.broadcasted_iota(jnp.int32, (1, 128), 1)
    slot = lane >> 5
    inside = ((lane & 31) >> 1) + TR * (lane & 1)

    @pl.loop(0, NT)
    def _(t):
        value = jnp.full((1, 128), -1, jnp.int32)
        for k in range(CAP):
            b = block_of[t * CAP + k]
            start = jnp.where(b >= 0, shift[jnp.maximum(b, 0)], -4096)
            value = jnp.where(slot == k, start + inside, value)
        koff_ref[pl.ds(t, 1), :] = value

    for copy in loads:
        copy.wait()

    @pl.loop(0, NT * CAP)
    def _(s):
        b = block_of[s]

        @pl.when(b >= 0)
        def _():
            pltpu.make_async_copy(held.at[:, b], z_ref.at[:, s], out_sem).start()

        @pl.when(b < 0)
        def _():
            pltpu.make_async_copy(zeros, z_ref.at[:, s], out_sem).start()

    pltpu.make_async_copy(z_ref, z_ref, out_sem).wait()


def sort_blocks(x, dest, shift):
    return pl.pallas_call(
        sort_kernel,
        out_shape=(
            jax.ShapeDtypeStruct((NQ, NT * CAP, BR, 2, 128), jnp.bfloat16),
            jax.ShapeDtypeStruct((NT, 128), jnp.int32),
        ),
        in_specs=[
            pl.BlockSpec(memory_space=pltpu.SMEM),
            pl.BlockSpec(memory_space=pltpu.SMEM),
            pl.BlockSpec(memory_space=pl.ANY),
        ],
        out_specs=(pl.BlockSpec(memory_space=pl.ANY), pl.BlockSpec(memory_space=pltpu.VMEM)),
        scratch_shapes=[
            pltpu.VMEM((NQ, BLK, BR, 2, 128), jnp.bfloat16),
            pltpu.VMEM((NQ, BR, 2, 128), jnp.bfloat16),
            pltpu.SMEM((NT,), jnp.int32),
            pltpu.SMEM((NT * CAP,), jnp.int32),
            pltpu.SemaphoreType.DMA((NQ,)),
            pltpu.SemaphoreType.DMA,
        ],
        name="sort_blocks",
    )(dest, shift, x)


def encode(total, out, rows):
    top = jnp.maximum(jnp.max(rows, axis=0, keepdims=True), 1e-30)
    power = jnp.clip(jnp.ceil(jnp.log2(top)), -100.0, 100.0)
    out[2 * TR :, :] = jnp.broadcast_to(power, (16, 128)).astype(jnp.int32).astype(jnp.int16)
    scale = jnp.exp2(-power)
    for i in range(4):
        v = total[i * 128 : (i + 1) * 128, :]
        y = jnp.abs(v) * scale
        y = y * lax.rsqrt(jnp.maximum(y, 1e-30))
        y = y * lax.rsqrt(jnp.maximum(y, 1e-15))
        m = (y * LEVELS + 0.5).astype(jnp.int32)
        out[i * 128 : (i + 1) * 128, :] = jnp.where(v < 0, -m, m).astype(jnp.int16)


def scale_of(msg):
    power = msg[2 * TR :, :].astype(jnp.int32).astype(jnp.float32)
    return jnp.exp2(power[0:1, :])


def decode(msg, scale, i):
    f = msg[i * 128 : (i + 1) * 128, :].astype(jnp.int32).astype(jnp.float32) * (1.0 / LEVELS)
    f = f * jnp.abs(f)
    f = f * jnp.abs(f)
    return f * scale


def main_kernel(
    z_ref, koff_ref, ep_ref, out_ref,
    got, kof, place, sent, came, total, fall0, fall1, prod, split, acc, bands, result,
    own_sem, xs_sem, xr_sem, zs_sem, zr_sem, ys_sem, yr_sem, cs_sem, cr_sem, ks_sem, kr_sem, out_sem,
):
    d = lax.axis_index("date")
    t = lax.axis_index("tile")
    y, core = d // 2, d % 2
    x, z = t // NZ, t % NZ
    partner = (y * 2 + 1 - core, t)

    def at_x(k):
        return (d, lax.rem(x + k, NX) * NZ + z)

    def at_z(k):
        return (d, x * NZ + lax.rem(z + k + NZ, NZ))

    def at_y(k):
        return (lax.rem(y + k, NY) * 2 + core, t)

    for q in range(NQ):
        @pl.loop(0, NZ)
        def _(j, q=q):
            for s in range(NX):
                got[q, j, s * KP + KS : (s + 1) * KP, :] = jnp.zeros((KP - KS, 128), jnp.bfloat16)

    barrier = pltpu.get_barrier_semaphore()
    peers = [at_x(1), at_x(2), at_x(3), at_z(1), at_z(-1), at_y(1), at_y(2), at_y(3), partner]
    for peer in peers:
        pl.semaphore_signal(barrier, 1, device_id=peer, device_id_type=MESH)
    pl.semaphore_wait(barrier, len(peers))

    def remote(src, dst, ssem, rsem, dev):
        return pltpu.make_async_remote_copy(
            src_ref=src, dst_ref=dst, send_sem=ssem, recv_sem=rsem, device_id=dev, device_id_type=MESH
        )

    def koff_copy(k):
        there = lax.rem(x + k, NX)
        return remote(
            koff_ref.at[pl.ds(pl.multiple_of(there * NZ, NZ), NZ)], kof.at[x],
            ks_sem.at[k - 1], kr_sem.at[k - 1], at_x(k),
        )

    def x_copy(q, k):
        there = lax.rem(x + k, NX)
        return remote(
            z_ref.at[q, pl.ds(there * NZ, NZ)], got.at[q, :, pl.ds(pl.multiple_of(x * KP, KP), KS)],
            xs_sem.at[q, k - 1], xr_sem.at[q, k - 1], at_x(k),
        )

    def own_copy(q):
        return pltpu.make_async_copy(
            z_ref.at[q, pl.ds(x * NZ, NZ)], got.at[q, :, pl.ds(pl.multiple_of(x * KP, KP), KS)],
            own_sem.at[q],
        )

    for k in (1, 3, 2):
        koff_copy(k).start()

    @pl.loop(0, NQ)
    def _(q):
        for k in (1, 3, 2):
            x_copy(q, k).start()
        own_copy(q).start()

    for half in range(2):
        i = lax.broadcasted_iota(jnp.int32, (256, 256), 0)
        j = lax.broadcasted_iota(jnp.int32, (256, 256), 1)
        near = jnp.abs((i & 127) + half * 128 - j) <= 7
        bands[half] = jnp.where(near, 1.0, 0.0).astype(jnp.bfloat16)
    prod[...] = jnp.zeros_like(prod)
    kof[x] = koff_ref[pl.ds(pl.multiple_of(x * NZ, NZ), NZ), :]
    for k in (1, 3, 2):
        koff_copy(k).wait()

    @pl.loop(0, NZ)
    def _(j):
        for s in range(NX):
            goal = kof[s, pl.ds(j, 1), :]
            for i in range(4):
                row = lax.broadcasted_iota(jnp.int32, (128, 128), 0) + i * 128
                hit = jnp.where(row == goal, 1.0, 0.0).astype(jnp.bfloat16)
                place[j, i * 128 : (i + 1) * 128, s * 128 : (s + 1) * 128] = hit

    def part(q, j, i):
        return jnp.dot(
            place[j, i * 128 : (i + 1) * 128, :], got[q, j], preferred_element_type=jnp.float32
        )

    def z_copy(q, n, way):
        dev = (d, x * NZ + lax.rem(z + way + NZ, NZ))
        return remote(sent.at[q, n], came.at[q, n], zs_sem.at[q, n], zr_sem.at[q, n], dev)

    def begin(q, way, dist, n):
        j = lax.rem(z + way * dist + NZ, NZ)
        top = jnp.zeros((8, 128), jnp.float32)
        for i in range(4):
            v = part(q, j, i)
            total[i * 128 : (i + 1) * 128, :] = v
            top = jnp.maximum(top, jnp.max(jnp.abs(v).reshape(16, 8, 128), axis=0))
        encode(total, sent.at[q, n], top)
        z_copy(q, n, way).start()

    def carry_on(q, way, dist, n):
        j = lax.rem(z + way * dist + NZ, NZ)
        z_copy(q, n - 1, way).wait_recv()
        msg = came.at[q, n - 1]
        scale = scale_of(msg)
        top = jnp.zeros((8, 128), jnp.float32)
        for i in range(4):
            v = part(q, j, i) + decode(msg, scale, i)
            total[i * 128 : (i + 1) * 128, :] = v
            top = jnp.maximum(top, jnp.max(jnp.abs(v).reshape(16, 8, 128), axis=0))
        encode(total, sent.at[q, n], top)
        z_copy(q, n, way).start()

    def way_of(q):
        return 1 - 2 * lax.rem(q, 2)

    def y_copy(fall, q, k):
        mine = fall.at[d * 4 + lax.rem(q, 4)]
        return remote(mine, mine, ys_sem.at[q, k - 1], yr_sem.at[q, k - 1], at_y(k))

    def core_copy(fall, q, k):
        from_d = lax.rem(y - k + NY, NY) * 2 + core
        field = fall.at[from_d * 4 + lax.rem(q, 4)]
        return remote(field, field, cs_sem.at[q, k], cr_sem.at[q, k], partner)

    def finish(q, fall):
        way = way_of(q)
        z_copy(q, 3, way).wait_recv()
        z_copy(q, 6, -way).wait_recv()
        one, two = came.at[q, 3], came.at[q, 6]
        s1, s2 = scale_of(one), scale_of(two)
        for i in range(4):
            v = part(q, z, i) + (decode(one, s1, i) + decode(two, s2, i))
            fall[d * 4 + lax.rem(q, 4), i * 128 : (i + 1) * 128, :] = v.astype(jnp.bfloat16)
        for k in (1, 3, 2):
            y_copy(fall, q, k).start()
        core_copy(fall, q, 0).start()

    def forward(q, fall):
        for k in (1, 3, 2):
            y_copy(fall, q, k).wait_recv()
            core_copy(fall, q, k).start()

    def arrive(q, fall):
        for k in range(NY):
            core_copy(fall, q, k).wait_recv()

    def out_copy(side):
        return pltpu.make_async_copy(
            result.reshape(2, TR, NP, 128).at[side],
            out_ref.at[:, :, pl.ds(side * 128, 128)],
            out_sem.at[side],
        )

    def boxes(half, fall):
        @pl.loop(0, NP)
        def _(p):
            a = ep_ref[d * NP + p, 0]
            e = ep_ref[d * NP + p, 1]
            for i in range(4):
                lo = i * 64
                u0 = fall[a, lo : lo + 64, :].astype(jnp.float32)
                u1 = fall[a, TR + lo : TR + lo + 64, :].astype(jnp.float32)
                v0 = fall[e, lo : lo + 64, :].astype(jnp.float32)
                v1 = fall[e, TR + lo : TR + lo + 64, :].astype(jnp.float32)
                prod[0, 8 + lo : 72 + lo, :] = u0 * v0 + u1 * v1
                prod[1, 8 + lo : 72 + lo, :] = u1 * v0 - u0 * v1
                prod[2, 8 + lo : 72 + lo, :] = u0 * u0 + u1 * u1
                prod[3, 8 + lo : 72 + lo, :] = v0 * v0 + v1 * v1
            for f in range(4):
                for i in range(4):
                    lo = i * 64
                    s = prod[f, 5 + lo : 69 + lo, :]
                    for k in range(1, 7):
                        s = s + prod[f, 5 + lo + k : 69 + lo + k, :]
                    high = s.astype(jnp.bfloat16)
                    split[f, lo : lo + 64, 0:128] = high
                    split[f, lo : lo + 64, 128:256] = (s - high.astype(jnp.float32)).astype(jnp.bfloat16)
            for f in range(4):
                r = jnp.dot(split[f], bands[half], preferred_element_type=jnp.float32)
                acc[p, f] = r if half == 0 else acc[p, f] + r
            if half == 1:
                for i in range(8):
                    lo = i * 32
                    re, im = acc[p, 0, lo : lo + 32, :], acc[p, 1, lo : lo + 32, :]
                    pa, pe = acc[p, 2, lo : lo + 32, :], acc[p, 3, lo : lo + 32, :]
                    c = jnp.sqrt(re * re + im * im) / jnp.sqrt(jnp.maximum(pa * pe, 1.0))
                    for side in range(2):
                        rows = pl.ds(side * NP * TR + lo * NP + p, 32, stride=NP)
                        result[rows, :] = c[:, side * 128 : (side + 1) * 128]

    @pl.loop(0, NQ + 6)
    def _(step):
        @pl.when(step < NQ)
        def _():
            q = step
            for k in (1, 3, 2):
                x_copy(q, k).wait_recv()
            own_copy(q).wait()
            begin(q, way_of(q), 4, 0)

        @pl.when((step >= 1) & (step < NQ + 1))
        def _():
            q = step - 1
            begin(q, -way_of(q), 3, 4)

        @pl.loop(0, 5)
        def _(i):
            short = i // 3
            h = i + 1 - 2 * short
            q = step - h

            @pl.when((q >= 0) & (q < NQ))
            def _():
                carry_on(q, way_of(q) * (1 - 2 * short), 4 - h, h + 3 * short)

        for half, fall in enumerate((fall0, fall1)):
            first = half * 4

            @pl.when((step >= first + 4) & (step < first + 8))
            def _(fall=fall):
                finish(step - 4, fall)

            @pl.when((step >= first + 5) & (step < first + 9))
            def _(fall=fall):
                forward(step - 5, fall)

            @pl.when((step >= first + 6) & (step < first + 10))
            def _(fall=fall):
                arrive(step - 6, fall)

        @pl.when(step == 9)
        def _():
            boxes(0, fall0)

    boxes(1, fall1)
    for side in range(2):
        out_copy(side).start()

    @pl.loop(0, NQ)
    def _(q):
        for k in (1, 3, 2):
            x_copy(q, k).wait_send()
        for n in range(7):
            z_copy(q, n, 1).wait_send()
        for k in (1, 2, 3):
            y_copy(fall0, q, k).wait_send()
        for k in range(NY):
            core_copy(fall0, q, k).wait_send()

    for side in range(2):
        out_copy(side).wait()


def main_call(z, koff, epochs):
    dma = pltpu.SemaphoreType.DMA
    field = pltpu.VMEM((32, 2 * TR, 128), jnp.bfloat16)
    return pl.pallas_call(
        main_kernel,
        out_shape=jax.ShapeDtypeStruct((TR, NP, 256), jnp.float32),
        in_specs=[
            pl.BlockSpec(memory_space=pl.ANY),
            pl.BlockSpec(memory_space=pltpu.VMEM),
            pl.BlockSpec(memory_space=pltpu.SMEM),
        ],
        out_specs=pl.BlockSpec(memory_space=pl.ANY),
        scratch_shapes=[
            pltpu.VMEM((NQ, NZ, NX * KP, 128), jnp.bfloat16),
            pltpu.VMEM((NX, NZ, 128), jnp.int32),
            pltpu.VMEM((NZ, 2 * TR, NX * KP), jnp.bfloat16),
            pltpu.VMEM((NQ, 7, MSG, 128), jnp.int16),
            pltpu.VMEM((NQ, 7, MSG, 128), jnp.int16),
            pltpu.VMEM((2 * TR, 128), jnp.float32),
            field,
            field,
            pltpu.VMEM((4, TR + 16, 128), jnp.float32),
            pltpu.VMEM((4, TR, 256), jnp.bfloat16),
            pltpu.VMEM((NP, 4, TR, 256), jnp.float32),
            pltpu.VMEM((2, 256, 256), jnp.bfloat16),
            pltpu.VMEM((2 * TR * NP, 128), jnp.float32),
            dma((NQ,)),
            dma((NQ, 3)), dma((NQ, 3)),
            dma((NQ, 7)), dma((NQ, 7)),
            dma((NQ, 3)), dma((NQ, 3)),
            dma((NQ, NY)), dma((NQ, NY)),
            dma((3,)), dma((3,)),
            dma((2,)),
        ],
        compiler_params=pltpu.CompilerParams(
            collective_id=0, has_side_effects=True, vmem_limit_bytes=62 * 2**20
        ),
        name="tiles_and_coherence",
    )(z, koff, epochs)


def local(radar_echoes, destination_panel, panel_line_shift, epoch_couples):
    z, koff = sort_blocks(radar_echoes, destination_panel[:, 0], panel_line_shift)
    z = z.reshape(NQ, NT, KS, 128)
    return main_call(z, koff, epoch_couples)


def solution(mesh):
    in_specs = (P("tile", None, "date", None, None), P("tile", None), P("tile"), P())
    out_specs = P("tile", "date", None)
    return jax.shard_map(local, mesh=mesh, in_specs=in_specs, out_specs=out_specs, check_vma=False)
```

time: 374 us -> 151 us (0.40)
  waiting for transfers between devices: 195 us -> 0 us
  Pallas kernels: 0 us -> 146 us
  other arithmetic: 68.7 us -> 0 us
  local copies, waits for them, and re-layouts: 62.9 us -> 4.43 us
  starting transfers between devices: 21.4 us -> 0 us
  between operations: 13.5 us -> 0.02 us
  matrix products: 11.3 us -> 0 us
    pallas_call x0 -> x2, Pallas kernels: none -> 146 us  [the longest x1 140 us: main_call(): pl.pallas_call(main_kernel, out_shape=jax.ShapeDtypeStruct((TR, NP, 256),...]
    all_to_all x2 -> x0, waiting for transfers between devices: 138 us -> none  [the longest x1 138 us: local(): lax.all_to_all(send_blocks, 'tile', split_axis=0, concat_axis=0, tiled=True)]
    all_gather x1 -> x0, waiting for transfers between devices: 56.9 us -> none  [local(): all_dates = lax.all_gather(panel_raster, 'date', axis=1, tiled=True)]
    div x1 -> x0, other arithmetic: 56.5 us -> none  [coherence_of(): jnp.sqrt(box_re * box_re + box_im * box_im)]
    reshape x4 -> x0, local copies, waits for them, and re-layouts: 31.6 us -> none  [the longest x1 11.1 us: local(): send_blocks.astype(jnp.bfloat16)]
    all_to_all x2 -> x0, starting transfers between devices: 21.2 us -> none  [the longest x1 11.9 us: local(): lax.all_to_all(send_offset, 'tile', split_axis=0, concat_axis=0, tiled=True)]
    gather x2 -> x0, local copies, waits for them, and re-layouts: 20.7 us -> none  [the longest x1 10.4 us: local(): second = jnp.take(padded, mine[:, 1], axis=1)]
    dot_general x2 -> x0, matrix products: 11.3 us -> none  [the longest x1 6.72 us: local(): jnp.dot(chooser.astype(jnp.bfloat16), serial_patches, preferred_element_t...]
  transfers between devices with their start and end apart: 3 -> 0, of which waited for: 2 -> 0; matrix products, arithmetic and copies ran while one was open for 7% -> 0% of each run, Pallas kernels for 0% -> 0%
where the time goes in v1:
time: 151 us
  Pallas kernels  146 us (97%)
  local copies, waits for them, and re-layouts  4.43 us (3%)
    pallas_call x1, Pallas kernels, main_call(): pl.pallas_call(main_kernel, out_shape=jax.ShapeDtypeStruct((TR, NP, 256),...  140 us
    pallas_call x1, Pallas kernels, sort_blocks(): pl.pallas_call(sort_kernel, out_shape=(jax.ShapeDtypeStruct((NQ, NT * CAP...  6.11 us
    unnamed x2, local copies, waits for them, and re-layouts  4.43 us

profile of v1, /device:TPU:1, one launch (start us, length us, event | category | flops | bytes accessed | tf_op | source)
XLA Modules:
  0.0 150.6 jit_solution(1561757220887262974)
XLA Ops:
  0.0 1.4 copy.5.ep_ref
  1.4 6.1 %sort_blocks.1 = (bf16[8,96,16,2,128]{4,3,2,1,0:T(2,128)(2,1)}, s32[32,128]{1,0:T(8,128)}) custom-call(s32[64]{0:T(128)} %bitcast.3, s32[64]{0:T(128)} %shift.1, bf16[64,16,4,2,256]{4,3,2,1,0:T(2,128)(2,1)} %x_ref.1), custom_call_target="tpu_custom_call" | custom-call | tf_op jit(solution)/shard_map/sort_blocks/pallas_call | solution.py:83
  7.5 140.0 %tiles_and_coherence.1 = f32[256,8,256]{2,1,0:T(8,128)} custom-call(bf16[8,32,96,128]{3,2,1,0:T(8,128)(2,1)} %bitcast.2, s32[32,128]{1,0:T(8,128)} %get-tuple-element.8.koff_ref, s32[64,2]{1,0:T(8,128)} %copy.5.ep_ref), custom_call_target="tpu_custom_call" | custom-call | tf_op jit(solution)/shard_map/tiles_and_coherence/pallas_call | solution.py:394
  147.5 3.0 %copy.7 = f32[256,8,256]{2,1,0:T(8,128)} copy(f32[256,8,256]{2,1,0:T(8,128)} %tiles_and_coherence.1) | data formatting | bytes 4194304

commit v2 on v1

--- a/solution.py
+++ b/solution.py
@@ -291,8 +291,8 @@
     def boxes(half, fall):
         @pl.loop(0, NP)
         def _(p):
-            a = ep_ref[d * NP + p, 0]
-            e = ep_ref[d * NP + p, 1]
+            a = ep_ref[0, d * NP + p]
+            e = ep_ref[1, d * NP + p]
             for i in range(4):
                 lo = i * 64
                 u0 = fall[a, lo : lo + 64, :].astype(jnp.float32)
@@ -320,12 +320,13 @@
                     lo = i * 32
                     re, im = acc[p, 0, lo : lo + 32, :], acc[p, 1, lo : lo + 32, :]
                     pa, pe = acc[p, 2, lo : lo + 32, :], acc[p, 3, lo : lo + 32, :]
-                    c = jnp.sqrt(re * re + im * im) / jnp.sqrt(jnp.maximum(pa * pe, 1.0))
+                    n = re * re + im * im
+                    c = n * lax.rsqrt(jnp.maximum(n, 1e-30)) * lax.rsqrt(jnp.maximum(pa * pe, 1.0))
                     for side in range(2):
                         rows = pl.ds(side * NP * TR + lo * NP + p, 32, stride=NP)
                         result[rows, :] = c[:, side * 128 : (side + 1) * 128]
 
-    @pl.loop(0, NQ + 6)
+    @pl.loop(0, NQ + 4)
     def _(step):
         @pl.when(step < NQ)
         def _():
@@ -334,38 +335,40 @@
                 x_copy(q, k).wait_recv()
             own_copy(q).wait()
             begin(q, way_of(q), 4, 0)
+            begin(q, -way_of(q), 3, 4)
 
         @pl.when((step >= 1) & (step < NQ + 1))
         def _():
             q = step - 1
-            begin(q, -way_of(q), 3, 4)
-
-        @pl.loop(0, 5)
-        def _(i):
-            short = i // 3
-            h = i + 1 - 2 * short
-            q = step - h
-
-            @pl.when((q >= 0) & (q < NQ))
-            def _():
-                carry_on(q, way_of(q) * (1 - 2 * short), 4 - h, h + 3 * short)
+            carry_on(q, way_of(q), 2, 2)
+            carry_on(q, -way_of(q), 2, 5)
 
         for half, fall in enumerate((fall0, fall1)):
             first = half * 4
 
+            @pl.when((step >= first + 2) & (step < first + 6))
+            def _(fall=fall):
+                finish(step - 2, fall)
+
+            @pl.when((step >= first + 3) & (step < first + 7))
+            def _(fall=fall):
+                forward(step - 3, fall)
+
             @pl.when((step >= first + 4) & (step < first + 8))
             def _(fall=fall):
-                finish(step - 4, fall)
-
-            @pl.when((step >= first + 5) & (step < first + 9))
-            def _(fall=fall):
-                forward(step - 5, fall)
-
-            @pl.when((step >= first + 6) & (step < first + 10))
-            def _(fall=fall):
-                arrive(step - 6, fall)
-
-        @pl.when(step == 9)
+                arrive(step - 4, fall)
+
+        @pl.when(step < NQ)
+        def _():
+            carry_on(step, way_of(step), 3, 1)
+
+        @pl.when((step >= 1) & (step < NQ + 1))
+        def _():
+            q = step - 1
+            carry_on(q, way_of(q), 1, 3)
+            carry_on(q, -way_of(q), 1, 6)
+
+        @pl.when(step == 8)
         def _():
             boxes(0, fall0)
 
@@ -423,7 +426,7 @@
             dma((2,)),
         ],
         compiler_params=pltpu.CompilerParams(
-            collective_id=0, has_side_effects=True, vmem_limit_bytes=62 * 2**20
+            collective_id=0, has_side_effects=True, vmem_limit_bytes=48 * 2**20
         ),
         name="tiles_and_coherence",
     )(z, koff, epochs)
@@ -432,7 +435,7 @@
 def local(radar_echoes, destination_panel, panel_line_shift, epoch_couples):
     z, koff = sort_blocks(radar_echoes, destination_panel[:, 0], panel_line_shift)
     z = z.reshape(NQ, NT, KS, 128)
-    return main_call(z, koff, epoch_couples)
+    return main_call(z, koff, epoch_couples.T)
 
 
 def solution(mesh):

time: 151 us -> 143 us (0.947)
  Pallas kernels: 146 us -> 140 us
  local copies, waits for them, and re-layouts: 4.43 us -> 2.04 us
    pallas_call x1, Pallas kernels: 140 us -> 134 us  [main_call(): pl.pallas_call(main_kernel, out_shape=jax.ShapeDtypeStruct((TR, NP, 256),...]
    unnamed x2 -> x5, local copies, waits for them, and re-layouts: 4.43 us -> 2.04 us
where the time goes in v2:
time: 143 us
  Pallas kernels  140 us (98%)
  local copies, waits for them, and re-layouts  2.04 us (1%)
    pallas_call x1, Pallas kernels, main_call(): pl.pallas_call(main_kernel, out_shape=jax.ShapeDtypeStruct((TR, NP, 256),...  134 us
    pallas_call x1, Pallas kernels, sort_blocks(): pl.pallas_call(sort_kernel, out_shape=(jax.ShapeDtypeStruct((NQ, NT * CAP...  6.23 us

profile of v2, /device:TPU:1, one launch (start us, length us, event | category | flops | bytes accessed | tf_op | source)
XLA Modules:
  0.0 142.5 jit_solution(12382037621652731622)
XLA Ops:
  0.0 0.0 copy-start.1
  0.0 6.2 %sort_blocks.1 = (bf16[8,96,16,2,128]{4,3,2,1,0:T(2,128)(2,1)}, s32[32,128]{1,0:T(8,128)}) custom-call(s32[64]{0:T(128)} %bitcast.5, s32[64]{0:T(128)} %shift.1, bf16[64,16,4,2,256]{4,3,2,1,0:T(2,128)(2,1)} %x_ref.1), custom_call_target="tpu_custom_call" | custom-call | tf_op jit(solution)/shard_map/sort_blocks/pallas_call | solution.py:83
  6.2 0.0 copy-done.1
  6.3 0.0 copy-start
  6.3 0.7 copy-done
  7.0 134.2 %tiles_and_coherence.1 = f32[256,8,256]{2,1,0:T(8,128)S(1)} custom-call(bf16[8,32,96,128]{3,2,1,0:T(8,128)(2,1)} %bitcast.4, s32[32,128]{1,0:T(8,128)S(1)} %copy-done, s32[2,64]{1,0:T(2,128)S(1)} %bitcast.3), custom_call_target="tpu_custom_call" | custom-call | tf_op jit(solution)/shard_map/tiles_and_coherence/pallas_call | solution.py:397
  141.2 1.3 copy.6
Async XLA Ops:
  0.0 6.2 %copy-start.1 = (s32[64,2]{0,1:T(2,128)S(1)}, s32[64,2]{0,1:T(2,128)}, u32[]{:S(2)}) copy-start(s32[64,2]{0,1:T(2,128)} %param.7) | copy-start | bytes 1540
  6.3 0.7 copy-start

commit v3 on v2

v3 whole, which is shorter than its diff:
```python
import functools

import jax
import jax.numpy as jnp
from jax import lax
from jax.experimental import pallas as pl
from jax.experimental.pallas import tpu as pltpu
from jax.sharding import PartitionSpec as P

NX, NZ, NY = 4, 8, 4
NT = NX * NZ
TR = 256
BR = 16
CAP = 3
BLK = 64
NQ = 8
KS = CAP * BR * 2
KP = 128
NP = 8
MSG = 2 * TR + 16
LEVELS = 32000.0
MESH = pl.DeviceIdType.MESH


def table_kernel(dest, shift, table, koff_ref, count):
    z = lax.rem(lax.axis_index("tile"), NZ)

    @pl.loop(0, NT)
    def _(t):
        count[t] = 0

    @pl.loop(0, 2 * NT * CAP)
    def _(s):
        table[s] = -1

    @pl.loop(0, BLK)
    def _(b):
        t = dest[b]
        k = count[t]
        count[t] = k + 1
        column, off = (t // NZ) * NZ, lax.rem(t, NZ) - z
        table[(column + ((off + 2) & 7)) * CAP + k] = b
        table[(NT + column + ((2 - off) & 7)) * CAP + k] = b

    lane = lax.broadcasted_iota(jnp.int32, (1, 128), 1)
    slot = lane >> 5
    inside = ((lane & 31) >> 1) + TR * (lane & 1)

    @pl.loop(0, 2 * NT)
    def _(t):
        value = jnp.full((1, 128), -1, jnp.int32)
        for k in range(CAP):
            b = table[t * CAP + k]
            start = jnp.where(b >= 0, shift[jnp.maximum(b, 0)], -4096)
            value = jnp.where(slot == k, start + inside, value)
        koff_ref[t] = value


def block_tables(dest, shift):
    smem = pl.BlockSpec(memory_space=pltpu.SMEM)
    return pl.pallas_call(
        table_kernel,
        out_shape=(
            jax.ShapeDtypeStruct((2 * NT * CAP,), jnp.int32),
            jax.ShapeDtypeStruct((2 * NT, 1, 128), jnp.int32),
        ),
        in_specs=[smem, smem],
        out_specs=(smem, pl.BlockSpec(memory_space=pltpu.VMEM)),
        scratch_shapes=[pltpu.SMEM((NT,), jnp.int32)],
        name="block_tables",
    )(dest, shift)


def encode(total, out, rows):
    top = jnp.maximum(jnp.max(rows, axis=0, keepdims=True), 1e-30)
    power = jnp.clip(jnp.ceil(jnp.log2(top)), -100.0, 100.0)
    out[2 * TR :, :] = jnp.broadcast_to(power, (16, 128)).astype(jnp.int32).astype(jnp.int16)
    scale = jnp.exp2(-power)
    for i in range(4):
        v = total[i * 128 : (i + 1) * 128, :]
        y = jnp.abs(v) * scale
        y = y * lax.rsqrt(jnp.maximum(y, 1e-30))
        y = y * lax.rsqrt(jnp.maximum(y, 1e-15))
        m = (y * LEVELS + 0.5).astype(jnp.int32)
        out[i * 128 : (i + 1) * 128, :] = jnp.where(v < 0, -m, m).astype(jnp.int16)


def scale_of(msg):
    power = msg[2 * TR :, :].astype(jnp.int32).astype(jnp.float32)
    return jnp.exp2(power[0:1, :])


def decode(msg, scale, i):
    f = msg[i * 128 : (i + 1) * 128, :].astype(jnp.int32).astype(jnp.float32) * (1.0 / LEVELS)
    f = f * jnp.abs(f)
    f = f * jnp.abs(f)
    return f * scale


def main_kernel(
    table, koff_ref, ep_ref, x_ref, out_ref,
    held, zb, got, kof, place, sent, came, total, fall0, fall1, prod, split, acc, bands, result,
    in_sem, own_sem, xs_sem, xr_sem, zs_sem, zr_sem, ys_sem, yr_sem, cs_sem, cr_sem, ks_sem, kr_sem, out_sem,
):
    d = lax.axis_index("date")
    t = lax.axis_index("tile")
    y, core = d // 2, lax.rem(d, 2)
    x, z = t // NZ, lax.rem(t, NZ)
    partner = (y * 2 + 1 - core, t)

    def at(dx, dz):
        return (d, lax.rem(x + dx, NX) * NZ + lax.rem(z + dz + NZ, NZ))

    def at_y(k):
        return (lax.rem(y + k, NY) * 2 + core, t)

    def load(q):
        half, date = divmod(q, 4)
        return pltpu.make_async_copy(
            x_ref.at[:, :, date, :, pl.ds(half * 128, 128)], held.at[pl.ds(q * BLK, BLK)], in_sem.at[q]
        )

    for q in range(NQ):
        load(q).start()

    @pl.loop(0, NQ)
    def _(q):
        for j in range(NZ):
            for s in range(NX):
                got[q, j, s * KP + KS : (s + 1) * KP, :] = jnp.zeros((KP - KS, 128), jnp.bfloat16)

    barrier = pltpu.get_barrier_semaphore()
    peers = [at(1, 0), at(2, 0), at(3, 0), at_y(1), at_y(2), at_y(3), partner]
    peers += [at(k, way) for k in range(NX) for way in (1, -1)]
    for peer in peers:
        pl.semaphore_signal(barrier, 1, device_id=peer, device_id_type=MESH)
    pl.semaphore_wait(barrier, len(peers))

    def remote(src, dst, ssem, rsem, dev):
        return pltpu.make_async_remote_copy(
            src_ref=src, dst_ref=dst, send_sem=ssem, recv_sem=rsem, device_id=dev, device_id_type=MESH
        )

    def way_of(q):
        return 1 - 2 * lax.rem(q, 2)

    def koff_copies(par):
        copies = []
        for k in (1, 3, 2):
            there = lax.rem(x + k, NX)
            copies.append(remote(
                koff_ref.at[pl.ds(par * NT + there * NZ, 6)], kof.at[par, x, pl.ds(0, 6)],
                ks_sem.at[par, k], kr_sem.at[par, k], at(k, 0),
            ))
        for m, way in ((6, 1 - 2 * par), (7, 2 * par - 1)):
            for k in range(NX):
                there, n = lax.rem(x + k, NX), 4 * (m - 5) + k
                copies.append(remote(
                    koff_ref.at[par * NT + there * NZ + m], kof.at[par, x, m],
                    ks_sem.at[par, n], kr_sem.at[par, n], at(k, way),
                ))
        return copies

    def x_copies(q):
        rows = pl.ds(pl.multiple_of(x * KP, KP), KS)
        copies = []
        for m, way in ((6, way_of(q)), (7, -way_of(q))):
            for k in range(NX):
                there, n = lax.rem(x + k, NX), 4 * (m - 5) + k
                copies.append(remote(
                    zb.at[q, there * NZ + m], got.at[q, m, rows],
                    xs_sem.at[q, n], xr_sem.at[q, n], at(k, way),
                ))
        for k in (1, 3, 2):
            there = lax.rem(x + k, NX)
            copies.append(remote(
                zb.at[q, pl.ds(there * NZ, 6)], got.at[q, pl.ds(0, 6), rows],
                xs_sem.at[q, k], xr_sem.at[q, k], at(k, 0),
            ))
        return copies

    def own_copy(q):
        return pltpu.make_async_copy(
            zb.at[q, pl.ds(x * NZ, 6)], got.at[q, pl.ds(0, 6), pl.ds(pl.multiple_of(x * KP, KP), KS)],
            own_sem.at[q],
        )

    for par in range(2):
        for copy in koff_copies(par):
            copy.start()
    for q in range(NQ):
        load(q).wait()

    blocks = held.reshape(NQ * BLK, 2 * BR, 128)

    def send_blocks(q):
        par = lax.rem(q, 2)

        @pl.loop(0, NT)
        def _(i):
            for k in range(CAP):
                b = table[(par * NT + i) * CAP + k]
                v = blocks[q * BLK + jnp.maximum(b, 0)]
                zb[q, i, k * 32 : (k + 1) * 32, :] = jnp.where(b >= 0, v, jnp.zeros_like(v))

        for copy in x_copies(q):
            copy.start()
        own_copy(q).start()

    def build(par):
        kof[par, x, 0:6] = koff_ref[pl.ds(par * NT + x * NZ, 6)]
        for copy in koff_copies(par):
            copy.wait()

        @pl.loop(0, NZ)
        def _(j):
            for s in range(NX):
                goal = kof[par, s, j]
                for i in range(4):
                    row = lax.broadcasted_iota(jnp.int32, (128, 128), 0) + i * 128
                    hit = jnp.where(row == goal, 1.0, 0.0).astype(jnp.bfloat16)
                    place[par, j, i * 128 : (i + 1) * 128, s * 128 : (s + 1) * 128] = hit

    @pl.loop(0, 3)
    def _(q):
        send_blocks(q)

    build(0)
    build(1)
    for half in range(2):
        i = lax.broadcasted_iota(jnp.int32, (256, 256), 0)
        j = lax.broadcasted_iota(jnp.int32, (256, 256), 1)
        near = jnp.abs((i & 127) + half * 128 - j) <= 7
        bands[half] = jnp.where(near, 1.0, 0.0).astype(jnp.bfloat16)
    prod[...] = jnp.zeros_like(prod)

    def part(q, j, i):
        return jnp.dot(
            place[lax.rem(q, 2), j, i * 128 : (i + 1) * 128, :], got[q, j],
            preferred_element_type=jnp.float32,
        )

    def z_copy(q, n, way):
        return remote(sent.at[q, n], came.at[q, n], zs_sem.at[q, n], zr_sem.at[q, n], at(0, way))

    def begin(q, way, j, n):
        top = jnp.zeros((8, 128), jnp.float32)
        for i in range(4):
            v = part(q, j[0], i) + part(q, j[1], i)
            total[i * 128 : (i + 1) * 128, :] = v
            top = jnp.maximum(top, jnp.max(jnp.abs(v).reshape(16, 8, 128), axis=0))
        encode(total, sent.at[q, n], top)
        z_copy(q, n, way).start()

    def carry_on(q, way, j, n):
        z_copy(q, n - 1, way).wait_recv()
        msg = came.at[q, n - 1]
        scale = scale_of(msg)
        top = jnp.zeros((8, 128), jnp.float32)
        for i in range(4):
            v = part(q, j, i) + decode(msg, scale, i)
            total[i * 128 : (i + 1) * 128, :] = v
            top = jnp.maximum(top, jnp.max(jnp.abs(v).reshape(16, 8, 128), axis=0))
        encode(total, sent.at[q, n], top)
        z_copy(q, n, way).start()

    def y_copy(fall, q, k):
        mine = fall.at[d * 4 + lax.rem(q, 4)]
        return remote(mine, mine, ys_sem.at[q, k - 1], yr_sem.at[q, k - 1], at_y(k))

    def core_copy(fall, q, k):
        from_d = lax.rem(y - k + NY, NY) * 2 + core
        field = fall.at[from_d * 4 + lax.rem(q, 4)]
        return remote(field, field, cs_sem.at[q, k], cr_sem.at[q, k], partner)

    def finish(q, fall):
        way = way_of(q)
        z_copy(q, 2, way).wait_recv()
        z_copy(q, 4, -way).wait_recv()
        one, two = came.at[q, 2], came.at[q, 4]
        s1, s2 = scale_of(one), scale_of(two)
        for i in range(4):
            v = part(q, 2, i) + (decode(one, s1, i) + decode(two, s2, i))
            fall[d * 4 + lax.rem(q, 4), i * 128 : (i + 1) * 128, :] = v.astype(jnp.bfloat16)
        for k in (1, 3, 2):
            y_copy(fall, q, k).start()
        core_copy(fall, q, 0).start()

    def forward(q, fall):
        for k in (1, 3, 2):
            y_copy(fall, q, k).wait_recv()
            core_copy(fall, q, k).start()

    def arrive(q, fall):
        for k in range(NY):
            core_copy(fall, q, k).wait_recv()

    def out_copy(side):
        return pltpu.make_async_copy(
            result.reshape(2, TR, NP, 128).at[side],
            out_ref.at[:, :, pl.ds(side * 128, 128)],
            out_sem.at[side],
        )

    def boxes(half, fall, first, number):
        @pl.loop(first, first + number)
        def _(p):
            a = ep_ref[0, d * NP + p]
            e = ep_ref[1, d * NP + p]
            for i in range(4):
                lo = i * 64
                u0 = fall[a, lo : lo + 64, :].astype(jnp.float32)
                u1 = fall[a, TR + lo : TR + lo + 64, :].astype(jnp.float32)
                v0 = fall[e, lo : lo + 64, :].astype(jnp.float32)
                v1 = fall[e, TR + lo : TR + lo + 64, :].astype(jnp.float32)
                prod[0, 8 + lo : 72 + lo, :] = u0 * v0 + u1 * v1
                prod[1, 8 + lo : 72 + lo, :] = u1 * v0 - u0 * v1
                prod[2, 8 + lo : 72 + lo, :] = u0 * u0 + u1 * u1
                prod[3, 8 + lo : 72 + lo, :] = v0 * v0 + v1 * v1
            for f in range(4):
                for i in range(4):
                    lo = i * 64
                    s = prod[f, 5 + lo : 69 + lo, :]
                    for k in range(1, 7):
                        s = s + prod[f, 5 + lo + k : 69 + lo + k, :]
                    high = s.astype(jnp.bfloat16)
                    split[f, lo : lo + 64, 0:128] = high
                    split[f, lo : lo + 64, 128:256] = (s - high.astype(jnp.float32)).astype(jnp.bfloat16)
            for f in range(4):
                r = jnp.dot(split[f], bands[half], preferred_element_type=jnp.float32)
                acc[p, f] = r if half == 0 else acc[p, f] + r
            if half == 1:
                for i in range(8):
                    lo = i * 32
                    re, im = acc[p, 0, lo : lo + 32, :], acc[p, 1, lo : lo + 32, :]
                    pa, pe = acc[p, 2, lo : lo + 32, :], acc[p, 3, lo : lo + 32, :]
                    n = re * re + im * im
                    c = n * lax.rsqrt(jnp.maximum(n, 1e-30)) * lax.rsqrt(jnp.maximum(pa * pe, 1.0))
                    for side in range(2):
                        rows = pl.ds(side * NP * TR + lo * NP + p, 32, stride=NP)
                        result[rows, :] = c[:, side * 128 : (side + 1) * 128]

    @pl.loop(0, NQ + 3)
    def _(step):
        @pl.when(step < NQ)
        def _():
            q = step
            way = way_of(q)
            for copy in x_copies(q):
                copy.wait_recv()
            own_copy(q).wait()
            begin(q, way, (5, 6), 0)
            begin(q, -way, (0, 7), 3)

        @pl.when((step >= 1) & (step < NQ + 1))
        def _():
            carry_on(step - 1, way_of(step - 1), 3, 2)

        @pl.when(step + 3 < NQ)
        def _():
            send_blocks(step + 3)

        for half, fall in enumerate((fall0, fall1)):
            first = half * 4

            @pl.when((step >= first + 2) & (step < first + 6))
            def _(fall=fall):
                forward(step - 2, fall)

            @pl.when((step >= first + 3) & (step < first + 7))
            def _(fall=fall):
                arrive(step - 3, fall)

        @pl.when(step < NQ)
        def _():
            way = way_of(step)
            carry_on(step, way, 4, 1)
            carry_on(step, -way, 1, 4)

        for half, fall in enumerate((fall0, fall1)):
            first = half * 4

            @pl.when((step >= first + 1) & (step < first + 5))
            def _(fall=fall):
                finish(step - 1, fall)

        @pl.when((step >= 6) & (step < 10))
        def _():
            boxes(0, fall0, (step - 6) * 2, 2)

    boxes(1, fall1, 0, NP)
    for side in range(2):
        out_copy(side).start()

    @pl.loop(0, NQ)
    def _(q):
        for copy in x_copies(q):
            copy.wait_send()
        for n in range(5):
            z_copy(q, n, 1).wait_send()
        for k in (1, 2, 3):
            y_copy(fall0, q, k).wait_send()
        for k in range(NY):
            core_copy(fall0, q, k).wait_send()

    for side in range(2):
        out_copy(side).wait()


def main_call(table, koff, epochs, x):
    dma = pltpu.SemaphoreType.DMA
    field = pltpu.VMEM((32, 2 * TR, 128), jnp.bfloat16)
    smem = pl.BlockSpec(memory_space=pltpu.SMEM)
    return pl.pallas_call(
        main_kernel,
        out_shape=jax.ShapeDtypeStruct((TR, NP, 256), jnp.float32),
        in_specs=[smem, pl.BlockSpec(memory_space=pltpu.VMEM), smem, pl.BlockSpec(memory_space=pl.ANY)],
        out_specs=pl.BlockSpec(memory_space=pl.ANY),
        scratch_shapes=[
            pltpu.VMEM((NQ * BLK, BR, 2, 128), jnp.bfloat16),
            pltpu.VMEM((NQ, NT, KS, 128), jnp.bfloat16),
            pltpu.VMEM((NQ, NZ, NX * KP, 128), jnp.bfloat16),
            pltpu.VMEM((2, NX, NZ, 1, 128), jnp.int32),
            pltpu.VMEM((2, NZ, 2 * TR, NX * KP), jnp.bfloat16),
            pltpu.VMEM((NQ, 5, MSG, 128), jnp.int16),
            pltpu.VMEM((NQ, 5, MSG, 128), jnp.int16),
            pltpu.VMEM((2 * TR, 128), jnp.float32),
            field,
            field,
            pltpu.VMEM((4, TR + 16, 128), jnp.float32),
            pltpu.VMEM((4, TR, 256), jnp.bfloat16),
            pltpu.VMEM((NP, 4, TR, 256), jnp.float32),
            pltpu.VMEM((2, 256, 256), jnp.bfloat16),
            pltpu.VMEM((2 * TR * NP, 128), jnp.float32),
            dma((NQ,)), dma((NQ,)),
            dma((NQ, 12)), dma((NQ, 12)),
            dma((NQ, 5)), dma((NQ, 5)),
            dma((NQ, 3)), dma((NQ, 3)),
            dma((NQ, NY)), dma((NQ, NY)),
            dma((2, 12)), dma((2, 12)),
            dma((2,)),
        ],
        compiler_params=pltpu.CompilerParams(
            collective_id=0, has_side_effects=True, vmem_limit_bytes=58 * 2**20
        ),
        name="tiles_and_coherence",
    )(table, koff, epochs, x)


def local(radar_echoes, destination_panel, panel_line_shift, epoch_couples):
    table, koff = block_tables(destination_panel[:, 0], panel_line_shift)
    return main_call(table, koff, epoch_couples.T, radar_echoes)


def solution(mesh):
    in_specs = (P("tile", None, "date", None, None), P("tile", None), P("tile"), P())
    out_specs = P("tile", "date", None)
    return jax.shard_map(local, mesh=mesh, in_specs=in_specs, out_specs=out_specs, check_vma=False)
```

time: 143 us -> 138 us (0.965)
  Pallas kernels: 140 us -> 133 us
    pallas_call x1, Pallas kernels: 134 us -> 128 us  [main_call(): pl.pallas_call(main_kernel, out_shape=jax.ShapeDtypeStruct((TR, NP, 256),...]
    unnamed x5 -> x1, local copies, waits for them, and re-layouts: 2.04 us -> 3.05 us
where the time goes in v3:
time: 138 us; the launch traced here: 136 us
  Pallas kernels  133 us (96%)
  local copies, waits for them, and re-layouts  3.05 us (2%)
    pallas_call x1, Pallas kernels, main_call(): pl.pallas_call(main_kernel, out_shape=jax.ShapeDtypeStruct((TR, NP, 256),...  128 us
    pallas_call x1, Pallas kernels, block_tables(): pl.pallas_call(table_kernel, out_shape=(jax.ShapeDtypeStruct((2 * NT * CA...  4.97 us
    unnamed x1, local copies, waits for them, and re-layouts  3.05 us

profile of v3, /device:TPU:1, one launch (start us, length us, event | category | flops | bytes accessed | tf_op | source)
XLA Modules:
  0.0 136.5 jit_solution(16852161371500542018)
XLA Ops:
  0.0 5.0 %block_tables.1 = (s32[192]{0:T(256)}, s32[64,1,128]{2,1,0:T(1,128)}) custom-call(s32[64]{0:T(128)} %bitcast.3, s32[64]{0:T(128)} %shift.1), custom_call_target="tpu_custom_call" | custom-call | tf_op jit(solution)/shard_map/block_tables/pallas_call | solution.py:61
  5.0 128.4 %tiles_and_coherence.1 = f32[256,8,256]{2,1,0:T(8,128)} custom-call(s32[192]{0:T(256)} %get-tuple-element.7.table, s32[64,1,128]{2,1,0:T(1,128)} %get-tuple-element.8.koff_ref, s32[2,64]{1,0:T(2,128)} %bitcast.2, bf16[64,16,4,2,256]{4,3,2,1,0:T(2,128)(2,1)} %x_ref.1), custom_call_target="tpu_custom_call" | custom-call | tf_op jit(solution)/shard_map/tiles_and_coherence/pallas_call | solution.py:414
  133.4 3.0 %copy.6 = f32[256,8,256]{2,1,0:T(8,128)} copy(f32[256,8,256]{2,1,0:T(8,128)} %tiles_and_coherence.1) | data formatting | bytes 4194304

commit v4 on v3

v4 whole, which is shorter than its diff:
```python
import functools

import jax
import jax.numpy as jnp
from jax import lax
from jax.experimental import pallas as pl
from jax.experimental.pallas import tpu as pltpu
from jax.sharding import PartitionSpec as P

NX, NZ, NY = 4, 8, 4
NT = NX * NZ
TR = 256
BR = 16
CAP = 3
BLK = 64
NQ = 8
KS = CAP * BR * 2
KP = 128
NP = 8
MSG = 2 * TR + 16
PIECE = TR + 16
SLOT = (5, 4, 2, 1, 6, 7, 0, 3)
LEVELS = 32000.0
MESH = pl.DeviceIdType.MESH


def power_of(top):
    return jnp.clip(jnp.ceil(jnp.log2(jnp.maximum(top, 1e-30))), -100.0, 100.0)


def encode(v, scale):
    y = jnp.abs(v) * scale
    y = y * lax.rsqrt(jnp.maximum(y, 1e-30))
    y = y * lax.rsqrt(jnp.maximum(y, 1e-15))
    m = (y * LEVELS + 0.5).astype(jnp.int32)
    return jnp.where(v < 0, -m, m).astype(jnp.int16)


def decode(code, scale):
    f = code.astype(jnp.int32).astype(jnp.float32) * (1.0 / LEVELS)
    f = f * jnp.abs(f)
    f = f * jnp.abs(f)
    return f * scale


def scale_of(power):
    return jnp.exp2(power.astype(jnp.int32).astype(jnp.float32)[0:1, :])


def main_kernel(
    dest_ref, shift_ref, ep_ref, x_ref, out_ref,
    table, listed, koff_ref, held, zb, got, kof, place, sent, came, total, fall0, fall1, prod, split, keep, bands, result,
    in_sem, own_sem, xs_sem, xr_sem, zs_sem, zr_sem, ys_sem, yr_sem, cs_sem, cr_sem, ks_sem, kr_sem, out_sem, table_sem,
):
    d = lax.axis_index("date")
    t = lax.axis_index("tile")
    y, core = d // 2, lax.rem(d, 2)
    x, z = t // NZ, lax.rem(t, NZ)
    partner = (y * 2 + 1 - core, t)

    def at(dx, dz):
        return (d, lax.rem(x + dx, NX) * NZ + lax.rem(z + dz + NZ, NZ))

    def at_y(k):
        return (lax.rem(y + k, NY) * 2 + core, t)

    def load(q):
        half, date = divmod(q, 4)
        return pltpu.make_async_copy(
            x_ref.at[:, :, date, :, pl.ds(half * 128, 128)], held.at[pl.ds(q * BLK, BLK)], in_sem.at[q]
        )

    for q in range(NQ):
        load(q).start()

    r = lax.broadcasted_iota(jnp.int32, (BLK, BLK), 0)
    c = lax.broadcasted_iota(jnp.int32, (BLK, BLK), 1)
    dest = dest_ref[...]
    along = jnp.broadcast_to(dest, (BLK, BLK)).astype(jnp.float32)
    shifts = jnp.broadcast_to(shift_ref[...], (BLK, BLK)).astype(jnp.float32)
    down = jnp.sum(jnp.where(r == c, along, 0.0), axis=1, keepdims=True)
    shift = jnp.sum(jnp.where(r == c, shifts, 0.0), axis=1, keepdims=True)
    rank = jnp.sum(jnp.where((down == along) & (c < r), 1.0, 0.0), axis=1, keepdims=True)
    lane = lax.broadcasted_iota(jnp.int32, (BLK, 128), 1)
    number = lax.broadcasted_iota(jnp.int32, (BLK, 128), 0)
    chosen = (lane >> 5).astype(jnp.float32) == rank
    off = (dest & (NZ - 1)) - z
    hit = jnp.zeros((BLK, BLK), jnp.float32)
    for par in range(2):
        turn = (off if par == 0 else -off) & (NZ - 1)
        index = par * NT + (dest - (dest & (NZ - 1)))
        for n, slot in enumerate(SLOT):
            index = index + jnp.where(turn == n, slot, 0)
        hit = hit + jnp.where(r == index, 1.0, 0.0)
    hit = hit.astype(jnp.bfloat16)
    first = jnp.where(chosen, (number + 1).astype(jnp.float32), 0.0).astype(jnp.bfloat16)
    second = jnp.where(chosen, shift + 1.0, 0.0).astype(jnp.bfloat16)
    listed[...] = jnp.dot(hit, first, preferred_element_type=jnp.float32).astype(jnp.int32) - 1
    start = jnp.dot(hit, second, preferred_element_type=jnp.float32).astype(jnp.int32)
    goals = jnp.where(start > 0, start - 1 + ((lane & 31) >> 1) + TR * (lane & 1), -1)
    for n in range(2 * NT):
        koff_ref[n] = goals[n : n + 1, :]
    table_copy = pltpu.make_async_copy(listed, table, table_sem)
    table_copy.start()

    @pl.loop(0, NQ)
    def _(q):
        for j in range(NZ):
            for s in range(NX):
                got[q, j, s * KP + KS : (s + 1) * KP, :] = jnp.zeros((KP - KS, 128), jnp.bfloat16)

    barrier = pltpu.get_barrier_semaphore()
    peers = [at(1, 0), at(2, 0), at(3, 0), at_y(1), at_y(2), at_y(3), partner]
    peers += [at(k, way) for k in range(NX) for way in (1, -1)]
    for peer in peers:
        pl.semaphore_signal(barrier, 1, device_id=peer, device_id_type=MESH)
    pl.semaphore_wait(barrier, len(peers))

    def remote(src, dst, ssem, rsem, dev):
        return pltpu.make_async_remote_copy(
            src_ref=src, dst_ref=dst, send_sem=ssem, recv_sem=rsem, device_id=dev, device_id_type=MESH
        )

    def way_of(q):
        return 1 - 2 * lax.rem(q, 2)

    def koff_copies(par):
        copies = []
        for k in (1, 3, 2):
            there = lax.rem(x + k, NX)
            copies.append(remote(
                koff_ref.at[pl.ds(par * NT + there * NZ, 6)], kof.at[par, x, pl.ds(0, 6)],
                ks_sem.at[par, k], kr_sem.at[par, k], at(k, 0),
            ))
        for m, way in ((6, 1 - 2 * par), (7, 2 * par - 1)):
            for k in range(NX):
                there, n = lax.rem(x + k, NX), 4 * (m - 5) + k
                copies.append(remote(
                    koff_ref.at[par * NT + there * NZ + m], kof.at[par, x, m],
                    ks_sem.at[par, n], kr_sem.at[par, n], at(k, way),
                ))
        return copies

    def x_group(q, g):
        rows = pl.ds(pl.multiple_of(x * KP, KP), KS)
        copies = []
        if g > 0:
            for k in (1, 3, 2):
                first, n = lax.rem(x + k, NX) * NZ + 2 * g - 2, 8 + 4 * g + k
                copies.append(remote(
                    zb.at[q, pl.ds(first, 2)], got.at[q, pl.ds(2 * g - 2, 2), rows],
                    xs_sem.at[q, n], xr_sem.at[q, n], at(k, 0),
                ))
            return copies
        for m, way in ((6, way_of(q)), (7, -way_of(q))):
            for k in range(NX):
                there, n = lax.rem(x + k, NX), 4 * (m - 5) + k
                copies.append(remote(
                    zb.at[q, there * NZ + m], got.at[q, m, rows],
                    xs_sem.at[q, n], xr_sem.at[q, n], at(k, way),
                ))
        return copies

    def own_copy(q):
        return pltpu.make_async_copy(
            zb.at[q, pl.ds(x * NZ, 6)], got.at[q, pl.ds(0, 6), pl.ds(pl.multiple_of(x * KP, KP), KS)],
            own_sem.at[q],
        )

    for par in range(2):
        for copy in koff_copies(par):
            copy.start()
    for q in range(NQ):
        load(q).wait()
    table_copy.wait()

    blocks = held.reshape(NQ * BLK, 2 * BR, 128)

    def send_blocks(q):
        par = lax.rem(q, 2)

        @pl.loop(0, NT)
        def _(i):
            for k in range(CAP):
                b = table[par * NT + i, k * 32]
                v = blocks[q * BLK + jnp.minimum(jnp.maximum(b, 0), BLK - 1)]
                zb[q, i, k * 32 : (k + 1) * 32, :] = jnp.where(b >= 0, v, jnp.zeros_like(v))

        for g in range(4):
            for copy in x_group(q, g):
                copy.start()
        own_copy(q).start()

    def build(par):
        kof[par, x, 0:6] = koff_ref[pl.ds(par * NT + x * NZ, 6)]
        for copy in koff_copies(par):
            copy.wait()

        @pl.loop(0, NZ)
        def _(j):
            for s in range(NX):
                goal = kof[par, s, j]
                for i in range(4):
                    row = lax.broadcasted_iota(jnp.int32, (128, 128), 0) + i * 128
                    hit = jnp.where(row == goal, 1.0, 0.0).astype(jnp.bfloat16)
                    place[par, j, i * 128 : (i + 1) * 128, s * 128 : (s + 1) * 128] = hit

    @pl.loop(0, 3)
    def _(q):
        send_blocks(q)

    build(0)
    build(1)
    for half in range(2):
        i = lax.broadcasted_iota(jnp.int32, (256, 256), 0)
        j = lax.broadcasted_iota(jnp.int32, (256, 256), 1)
        near = jnp.abs((i & 127) + half * 128 - j) <= 7
        bands[half] = jnp.where(near, 1.0, 0.0).astype(jnp.bfloat16)
    prod[...] = jnp.zeros_like(prod)

    def part(q, j, i):
        return jnp.dot(
            place[lax.rem(q, 2), j, i * 128 : (i + 1) * 128, :], got[q, j],
            preferred_element_type=jnp.float32,
        )

    def z_copy(q, n, h, way):
        piece = pl.ds(h * PIECE, PIECE if h == 0 else TR)
        return remote(
            sent.at[q, n, piece], came.at[q, n, piece], zs_sem.at[q, 2 * n + h], zr_sem.at[q, 2 * n + h], at(0, way)
        )

    def own_part(q, slots, at_total):
        top = jnp.zeros((8, 128), jnp.float32)
        for i in range(4):
            v = part(q, slots[0], i)
            for slot in slots[1:]:
                v = v + part(q, slot, i)
            total[at_total, i * 128 : (i + 1) * 128, :] = v
            top = jnp.maximum(top, jnp.max(jnp.abs(v).reshape(16, 8, 128), axis=0))
        return jnp.max(top, axis=0, keepdims=True)

    def hop(q, units):
        tops = [own_part(q, slots, u) for u, (_, slots, _, _) in enumerate(units)]
        scales = [None] * len(units)
        for h in range(2):
            for u, (way, _, taken, n) in enumerate(units):
                if taken is not None:
                    z_copy(q, taken, h, way).wait_recv()
                if h == 0:
                    arrived = None
                    if taken is not None:
                        arrived = scale_of(came[q, taken, 2 * 128 : PIECE, :])
                        tops[u] = tops[u] + arrived
                    power = power_of(tops[u])
                    sent[q, n, 2 * 128 : PIECE, :] = (
                        jnp.broadcast_to(power, (16, 128)).astype(jnp.int32).astype(jnp.int16)
                    )
                    scales[u] = (arrived, jnp.exp2(-power))
                arrived, scale = scales[u]
                for part_no in range(2):
                    i = part_no * 2 + h
                    rows = slice(h * PIECE + part_no * 128, h * PIECE + part_no * 128 + 128)
                    v = total[u, i * 128 : (i + 1) * 128, :]
                    if taken is not None:
                        v = v + decode(came[q, taken, rows, :], arrived)
                    sent[q, n, rows, :] = encode(v, scale)
                z_copy(q, n, h, way).start()

    def y_copy(fall, q, k, h):
        mine = fall.at[d * 4 + lax.rem(q, 4), :, pl.ds(h * 128, 128)]
        n = 2 * k - 2 + h
        return remote(mine, mine, ys_sem.at[q, n], yr_sem.at[q, n], at_y(k))

    def core_copy(fall, q, k, h):
        from_d = lax.rem(y - k + NY, NY) * 2 + core
        field = fall.at[from_d * 4 + lax.rem(q, 4), :, pl.ds(h * 128, 128)]
        return remote(field, field, cs_sem.at[q, 2 * k + h], cr_sem.at[q, 2 * k + h], partner)

    def finish(q, fall):
        way = way_of(q)
        own_part(q, (5,), 0)
        scales = [None, None]
        for h in range(2):
            for u, (n, w) in enumerate(((2, way), (4, -way))):
                z_copy(q, n, h, w).wait_recv()
                if h == 0:
                    scales[u] = scale_of(came[q, n, 2 * 128 : PIECE, :])
            for part_no in range(2):
                i = part_no * 2 + h
                rows = slice(h * PIECE + part_no * 128, h * PIECE + part_no * 128 + 128)
                v = total[0, i * 128 : (i + 1) * 128, :]
                v = v + (decode(came[q, 2, rows, :], scales[0]) + decode(came[q, 4, rows, :], scales[1]))
                fall[d * 4 + lax.rem(q, 4), part_no, h * 128 : (h + 1) * 128, :] = v.astype(jnp.bfloat16)
            for k in (1, 3, 2):
                y_copy(fall, q, k, h).start()
            core_copy(fall, q, 0, h).start()

    def forward(q, fall):
        for h in range(2):
            for k in (1, 3, 2):
                y_copy(fall, q, k, h).wait_recv()
                core_copy(fall, q, k, h).start()

    def arrive(q, fall):
        for h in range(2):
            for k in range(NY):
                core_copy(fall, q, k, h).wait_recv()

    def out_copy(side):
        return pltpu.make_async_copy(
            result.reshape(2, TR, NP, 128).at[side],
            out_ref.at[:, :, pl.ds(side * 128, 128)],
            out_sem.at[side],
        )

    def boxes(half, fall, first, number):
        @pl.loop(first, first + number)
        def _(p):
            a = ep_ref[0, d * NP + p]
            e = ep_ref[1, d * NP + p]
            for i in range(4):
                lo = i * 64
                u0 = fall[a, 0, lo : lo + 64, :].astype(jnp.float32)
                u1 = fall[a, 1, lo : lo + 64, :].astype(jnp.float32)
                v0 = fall[e, 0, lo : lo + 64, :].astype(jnp.float32)
                v1 = fall[e, 1, lo : lo + 64, :].astype(jnp.float32)
                prod[0, 8 + lo : 72 + lo, :] = u0 * v0 + u1 * v1
                prod[1, 8 + lo : 72 + lo, :] = u1 * v0 - u0 * v1
                prod[2, 8 + lo : 72 + lo, :] = u0 * u0 + u1 * u1
                prod[3, 8 + lo : 72 + lo, :] = v0 * v0 + v1 * v1
            for f in range(4):
                for i in range(4):
                    lo = i * 64
                    s = prod[f, 5 + lo : 69 + lo, :]
                    for k in range(1, 7):
                        s = s + prod[f, 5 + lo + k : 69 + lo + k, :]
                    high = s.astype(jnp.bfloat16)
                    low = (s - high.astype(jnp.float32)).astype(jnp.bfloat16)
                    if half == 0:
                        keep[p, f, lo : lo + 64, 0:128] = high
                        keep[p, f, lo : lo + 64, 128:256] = low
                    else:
                        split[f, lo : lo + 64, 0:128] = high
                        split[f, lo : lo + 64, 128:256] = low
            if half == 1:
                for i in range(4):
                    lo = i * 64
                    re, im, pa, pe = [
                        jnp.dot(keep[p, f, lo : lo + 64, :], bands[0], preferred_element_type=jnp.float32)
                        + jnp.dot(split[f, lo : lo + 64, :], bands[1], preferred_element_type=jnp.float32)
                        for f in range(4)
                    ]
                    n = re * re + im * im
                    c = n * lax.rsqrt(jnp.maximum(n, 1e-30)) * lax.rsqrt(jnp.maximum(pa * pe, 1.0))
                    for side in range(2):
                        rows = pl.ds(side * NP * TR + lo * NP + p, 64, stride=NP)
                        result[rows, :] = c[:, side * 128 : (side + 1) * 128]

    @pl.loop(0, NQ + 3)
    def _(step):
        @pl.when(step < NQ)
        def _():
            for copy in x_group(step, 0) + x_group(step, 1):
                copy.wait_recv()
            own_copy(step).wait()
            hop(step, ((way_of(step), (1, 6), None, 0), (-way_of(step), (0, 7), None, 3)))

        @pl.when((step >= 1) & (step < NQ + 1))
        def _():
            for copy in x_group(step - 1, 3):
                copy.wait_recv()
            hop(step - 1, ((way_of(step - 1), (4,), 1, 2),))

        @pl.when(step + 3 < NQ)
        def _():
            send_blocks(step + 3)

        for half, fall in enumerate((fall0, fall1)):
            first = half * 4

            @pl.when((step >= first + 2) & (step < first + 6))
            def _(fall=fall):
                forward(step - 2, fall)

            @pl.when((step >= first + 3) & (step < first + 7))
            def _(fall=fall):
                arrive(step - 3, fall)

        @pl.when(step < NQ)
        def _():
            for copy in x_group(step, 2):
                copy.wait_recv()
            hop(step, ((way_of(step), (2,), 0, 1), (-way_of(step), (3,), 3, 4)))

        for half, fall in enumerate((fall0, fall1)):
            first = half * 4

            @pl.when((step >= first + 1) & (step < first + 5))
            def _(fall=fall):
                finish(step - 1, fall)

        @pl.when((step >= 6) & (step < 10))
        def _():
            boxes(0, fall0, (step - 6) * 2, 2)

    boxes(1, fall1, 0, NP)
    for side in range(2):
        out_copy(side).start()

    @pl.loop(0, NQ)
    def _(q):
        for g in range(4):
            for copy in x_group(q, g):
                copy.wait_send()
        for h in range(2):
            for n in range(5):
                z_copy(q, n, h, 1).wait_send()
            for k in (1, 2, 3):
                y_copy(fall0, q, k, h).wait_send()
            for k in range(NY):
                core_copy(fall0, q, k, h).wait_send()

    for side in range(2):
        out_copy(side).wait()


def main_call(dest, shift, epochs, x):
    dma = pltpu.SemaphoreType.DMA
    field = pltpu.VMEM((32, 2, TR, 128), jnp.bfloat16)
    vmem = pl.BlockSpec(memory_space=pltpu.VMEM)
    return pl.pallas_call(
        main_kernel,
        out_shape=jax.ShapeDtypeStruct((TR, NP, 256), jnp.float32),
        in_specs=[vmem, vmem, pl.BlockSpec(memory_space=pltpu.SMEM), pl.BlockSpec(memory_space=pl.ANY)],
        out_specs=pl.BlockSpec(memory_space=pl.ANY),
        scratch_shapes=[
            pltpu.SMEM((2 * NT, 128), jnp.int32),
            pltpu.VMEM((2 * NT, 128), jnp.int32),
            pltpu.VMEM((2 * NT, 1, 128), jnp.int32),
            pltpu.VMEM((NQ * BLK, BR, 2, 128), jnp.bfloat16),
            pltpu.VMEM((NQ, NT, KS, 128), jnp.bfloat16),
            pltpu.VMEM((NQ, NZ, NX * KP, 128), jnp.bfloat16),
            pltpu.VMEM((2, NX, NZ, 1, 128), jnp.int32),
            pltpu.VMEM((2, NZ, 2 * TR, NX * KP), jnp.bfloat16),
            pltpu.VMEM((NQ, 5, MSG, 128), jnp.int16),
            pltpu.VMEM((NQ, 5, MSG, 128), jnp.int16),
            pltpu.VMEM((2, 2 * TR, 128), jnp.float32),
            field,
            field,
            pltpu.VMEM((4, TR + 16, 128), jnp.float32),
            pltpu.VMEM((4, TR, 256), jnp.bfloat16),
            pltpu.VMEM((NP, 4, TR, 256), jnp.bfloat16),
            pltpu.VMEM((2, 256, 256), jnp.bfloat16),
            pltpu.VMEM((2 * TR * NP, 128), jnp.float32),
            dma((NQ,)), dma((NQ,)),
            dma((NQ, 24)), dma((NQ, 24)),
            dma((NQ, 10)), dma((NQ, 10)),
            dma((NQ, 6)), dma((NQ, 6)),
            dma((NQ, 2 * NY)), dma((NQ, 2 * NY)),
            dma((2, 12)), dma((2, 12)),
            dma((2,)),
            dma,
        ],
        compiler_params=pltpu.CompilerParams(
            collective_id=0, has_side_effects=True, vmem_limit_bytes=53 * 2**20
        ),
        name="tiles_and_coherence",
    )(dest, shift, epochs, x)


def local(radar_echoes, destination_panel, panel_line_shift, epoch_couples):
    dest, shift = destination_panel.reshape(1, BLK), panel_line_shift.reshape(1, BLK)
    return main_call(dest, shift, epoch_couples.T, radar_echoes)


def solution(mesh):
    in_specs = (P("tile", None, "date", None, None), P("tile", None), P("tile"), P())
    out_specs = P("tile", "date", None)
    return jax.shard_map(local, mesh=mesh, in_specs=in_specs, out_specs=out_specs, check_vma=False)
```

time: 138 us -> 132 us (0.957); the launches traced: 136 us -> 132 us
  Pallas kernels: 133 us -> 127 us
  local copies, waits for them, and re-layouts: 3.05 us -> 5.03 us
    pallas_call x1 -> x0, Pallas kernels: 4.97 us -> none  [block_tables(): pl.pallas_call(table_kernel, out_shape=(jax.ShapeDtypeStruct((2 * NT * CA...]
    unnamed x1 -> x7, local copies, waits for them, and re-layouts: 3.05 us -> 5.03 us
    pallas_call x1, Pallas kernels: 128 us -> 127 us  [main_call(): pl.pallas_call(main_kernel, out_shape=jax.ShapeDtypeStruct((TR, NP, 256),...]
where the time goes in v4:
time: 132 us
  Pallas kernels  127 us (96%)
  local copies, waits for them, and re-layouts  5.03 us (4%)
    pallas_call x1, Pallas kernels, main_call(): pl.pallas_call(main_kernel, out_shape=jax.ShapeDtypeStruct((TR, NP, 256),...  127 us
    unnamed x7, local copies, waits for them, and re-layouts  5.03 us

profile of v4, /device:TPU:1, one launch (start us, length us, event | category | flops | bytes accessed | tf_op | source)
XLA Modules:
  0.0 131.9 jit_solution(1752156477398745493)
XLA Ops:
  0.0 0.0 copy-start
  0.0 0.7 copy-done
  0.7 0.0 copy-start.1
  0.7 0.7 copy-done.1
  1.3 0.0 copy-start.2
  1.3 0.7 copy-done.2
  2.0 126.9 %tiles_and_coherence.1 = f32[256,8,256]{2,1,0:T(8,128)} custom-call(s32[1,64]{1,0:T(1,128)S(1)} %bitcast.4, s32[1,64]{1,0:T(1,128)S(1)} %bitcast.5, s32[2,64]{1,0:T(2,128)S(1)} %bitcast.3, bf16[64,16,4,2,256]{4,3,2,1,0:T(2,128)(2,1)} %x_ref.1), custom_call_target="tpu_custom_call" | custom-call | tf_op jit(solution)/shard_map/tiles_and_coherence/pallas_call | solution.py:432
  128.9 3.0 %copy.6 = f32[256,8,256]{2,1,0:T(8,128)} copy(f32[256,8,256]{2,1,0:T(8,128)} %tiles_and_coherence.1) | data formatting | bytes 4194304
Async XLA Ops:
  0.0 0.7 copy-start
  0.7 0.7 copy-start.1
  1.3 0.7 copy-start.2

commit v5 on v4

--- a/solution.py
+++ b/solution.py
@@ -49,7 +49,7 @@
 
 def main_kernel(
     dest_ref, shift_ref, ep_ref, x_ref, out_ref,
-    table, listed, koff_ref, held, zb, got, kof, place, sent, came, total, fall0, fall1, prod, split, keep, bands, result,
+    table, listed, koff_ref, held, zb, got, kof, place, sent, came, total, fall0, fall1, prod, split, acc, bands, result,
     in_sem, own_sem, xs_sem, xr_sem, zs_sem, zr_sem, ys_sem, yr_sem, cs_sem, cr_sem, ks_sem, kr_sem, out_sem, table_sem,
 ):
     d = lax.axis_index("date")
@@ -73,6 +73,17 @@
     for q in range(NQ):
         load(q).start()
 
+    @pl.loop(0, NQ)
+    def _(q):
+        for j in range(NZ):
+            for s in range(NX):
+                got[q, j, s * KP + KS : (s + 1) * KP, :] = jnp.zeros((KP - KS, 128), jnp.bfloat16)
+
+    barrier = pltpu.get_barrier_semaphore()
+    peers = [at(1, 0), at(2, 0), at(3, 0), at_y(1), at_y(2), at_y(3), partner]
+    peers += [at(k, way) for k in range(NX) for way in (1, -1)]
+    for peer in peers:
+        pl.semaphore_signal(barrier, 1, device_id=peer, device_id_type=MESH)
     r = lax.broadcasted_iota(jnp.int32, (BLK, BLK), 0)
     c = lax.broadcasted_iota(jnp.int32, (BLK, BLK), 1)
     dest = dest_ref[...]
@@ -103,17 +114,6 @@
     table_copy = pltpu.make_async_copy(listed, table, table_sem)
     table_copy.start()
 
-    @pl.loop(0, NQ)
-    def _(q):
-        for j in range(NZ):
-            for s in range(NX):
-                got[q, j, s * KP + KS : (s + 1) * KP, :] = jnp.zeros((KP - KS, 128), jnp.bfloat16)
-
-    barrier = pltpu.get_barrier_semaphore()
-    peers = [at(1, 0), at(2, 0), at(3, 0), at_y(1), at_y(2), at_y(3), partner]
-    peers += [at(k, way) for k in range(NX) for way in (1, -1)]
-    for peer in peers:
-        pl.semaphore_signal(barrier, 1, device_id=peer, device_id_type=MESH)
     pl.semaphore_wait(barrier, len(peers))
 
     def remote(src, dst, ssem, rsem, dev):
@@ -337,24 +337,19 @@
                         s = s + prod[f, 5 + lo + k : 69 + lo + k, :]
                     high = s.astype(jnp.bfloat16)
                     low = (s - high.astype(jnp.float32)).astype(jnp.bfloat16)
-                    if half == 0:
-                        keep[p, f, lo : lo + 64, 0:128] = high
-                        keep[p, f, lo : lo + 64, 128:256] = low
-                    else:
-                        split[f, lo : lo + 64, 0:128] = high
-                        split[f, lo : lo + 64, 128:256] = low
+                    split[f, lo : lo + 64, 0:128] = high
+                    split[f, lo : lo + 64, 128:256] = low
+            for f in range(4):
+                r = jnp.dot(split[f], bands[half], preferred_element_type=jnp.float32)
+                acc[p, f] = r if half == 0 else acc[p, f] + r
             if half == 1:
-                for i in range(4):
-                    lo = i * 64
-                    re, im, pa, pe = [
-                        jnp.dot(keep[p, f, lo : lo + 64, :], bands[0], preferred_element_type=jnp.float32)
-                        + jnp.dot(split[f, lo : lo + 64, :], bands[1], preferred_element_type=jnp.float32)
-                        for f in range(4)
-                    ]
+                for i in range(8):
+                    lo = i * 32
+                    re, im, pa, pe = [acc[p, f, lo : lo + 32, :] for f in range(4)]
                     n = re * re + im * im
                     c = n * lax.rsqrt(jnp.maximum(n, 1e-30)) * lax.rsqrt(jnp.maximum(pa * pe, 1.0))
                     for side in range(2):
-                        rows = pl.ds(side * NP * TR + lo * NP + p, 64, stride=NP)
+                        rows = pl.ds(side * NP * TR + lo * NP + p, 32, stride=NP)
                         result[rows, :] = c[:, side * 128 : (side + 1) * 128]
 
     @pl.loop(0, NQ + 3)
@@ -400,9 +395,9 @@
             def _(fall=fall):
                 finish(step - 1, fall)
 
-        @pl.when((step >= 6) & (step < 10))
+        @pl.when((step == 6) | (step == 8))
         def _():
-            boxes(0, fall0, (step - 6) * 2, 2)
+            boxes(0, fall0, (step - 6) * 2, 4)
 
     boxes(1, fall1, 0, NP)
     for side in range(2):
@@ -450,7 +445,7 @@
             field,
             pltpu.VMEM((4, TR + 16, 128), jnp.float32),
             pltpu.VMEM((4, TR, 256), jnp.bfloat16),
-            pltpu.VMEM((NP, 4, TR, 256), jnp.bfloat16),
+            pltpu.VMEM((NP, 4, TR, 256), jnp.float32),
             pltpu.VMEM((2, 256, 256), jnp.bfloat16),
             pltpu.VMEM((2 * TR * NP, 128), jnp.float32),
             dma((NQ,)), dma((NQ,)),
@@ -463,7 +458,7 @@
             dma,
         ],
         compiler_params=pltpu.CompilerParams(
-            collective_id=0, has_side_effects=True, vmem_limit_bytes=53 * 2**20
+            collective_id=0, has_side_effects=True, vmem_limit_bytes=58 * 2**20
         ),
         name="tiles_and_coherence",
     )(dest, shift, epochs, x)

time: 132 us -> 129 us (0.977)
  local copies, waits for them, and re-layouts: 5.03 us -> 3.05 us
    unnamed x7 -> x1, local copies, waits for them, and re-layouts: 5.03 us -> 3.05 us
where the time goes in v5:
time: 129 us
  Pallas kernels  126 us (98%)
  local copies, waits for them, and re-layouts  3.05 us (2%)
    pallas_call x1, Pallas kernels, main_call(): pl.pallas_call(main_kernel, out_shape=jax.ShapeDtypeStruct((TR, NP, 256),...  126 us
    unnamed x1, local copies, waits for them, and re-layouts  3.05 us

profile of v5, /device:TPU:1, one launch (start us, length us, event | category | flops | bytes accessed | tf_op | source)
XLA Modules:
  0.0 128.6 jit_solution(7991972208721664914)
XLA Ops:
  0.0 125.6 %tiles_and_coherence.1 = f32[256,8,256]{2,1,0:T(8,128)} custom-call(s32[1,64]{1,0:T(1,128)} %bitcast.4, s32[1,64]{1,0:T(1,128)} %bitcast.5, s32[2,64]{1,0:T(2,128)} %bitcast.3, bf16[64,16,4,2,256]{4,3,2,1,0:T(2,128)(2,1)} %x_ref.1), custom_call_target="tpu_custom_call" | custom-call | tf_op jit(solution)/shard_map/tiles_and_coherence/pallas_call | solution.py:427
  125.6 3.0 %copy.6 = f32[256,8,256]{2,1,0:T(8,128)} copy(f32[256,8,256]{2,1,0:T(8,128)} %tiles_and_coherence.1) | data formatting | bytes 4194304

commit v6 on v5

--- a/solution.py
+++ b/solution.py
@@ -126,7 +126,7 @@
 
     def koff_copies(par):
         copies = []
-        for k in (1, 3, 2):
+        for k in (2, 1, 3):
             there = lax.rem(x + k, NX)
             copies.append(remote(
                 koff_ref.at[pl.ds(par * NT + there * NZ, 6)], kof.at[par, x, pl.ds(0, 6)],
@@ -145,7 +145,7 @@
         rows = pl.ds(pl.multiple_of(x * KP, KP), KS)
         copies = []
         if g > 0:
-            for k in (1, 3, 2):
+            for k in (2, 1, 3):
                 first, n = lax.rem(x + k, NX) * NZ + 2 * g - 2, 8 + 4 * g + k
                 copies.append(remote(
                     zb.at[q, pl.ds(first, 2)], got.at[q, pl.ds(2 * g - 2, 2), rows],
@@ -292,13 +292,13 @@
                 v = total[0, i * 128 : (i + 1) * 128, :]
                 v = v + (decode(came[q, 2, rows, :], scales[0]) + decode(came[q, 4, rows, :], scales[1]))
                 fall[d * 4 + lax.rem(q, 4), part_no, h * 128 : (h + 1) * 128, :] = v.astype(jnp.bfloat16)
-            for k in (1, 3, 2):
+            for k in (2, 1, 3):
                 y_copy(fall, q, k, h).start()
             core_copy(fall, q, 0, h).start()
 
     def forward(q, fall):
         for h in range(2):
-            for k in (1, 3, 2):
+            for k in (2, 1, 3):
                 y_copy(fall, q, k, h).wait_recv()
                 core_copy(fall, q, k, h).start()
 

time: 129 us -> 128 us (level)
  no operation moved by 1% of the time
where the time goes in v6:
time: 128 us
  Pallas kernels  125 us (98%)
  local copies, waits for them, and re-layouts  3.05 us (2%)
    pallas_call x1, Pallas kernels, main_call(): pl.pallas_call(main_kernel, out_shape=jax.ShapeDtypeStruct((TR, NP, 256),...  125 us
    unnamed x1, local copies, waits for them, and re-layouts  3.05 us

profile of v6, /device:TPU:1, one launch (start us, length us, event | category | flops | bytes accessed | tf_op | source)
XLA Modules:
  0.0 127.8 jit_solution(13599939166537198537)
XLA Ops:
  0.0 124.7 %tiles_and_coherence.1 = f32[256,8,256]{2,1,0:T(8,128)} custom-call(s32[1,64]{1,0:T(1,128)} %bitcast.4, s32[1,64]{1,0:T(1,128)} %bitcast.5, s32[2,64]{1,0:T(2,128)} %bitcast.3, bf16[64,16,4,2,256]{4,3,2,1,0:T(2,128)(2,1)} %x_ref.1), custom_call_target="tpu_custom_call" | custom-call | tf_op jit(solution)/shard_map/tiles_and_coherence/pallas_call | solution.py:427
  124.7 3.0 %copy.6 = f32[256,8,256]{2,1,0:T(8,128)} copy(f32[256,8,256]{2,1,0:T(8,128)} %tiles_and_coherence.1) | data formatting | bytes 4194304

commit v7 on v6

--- a/solution.py
+++ b/solution.py
@@ -49,7 +49,7 @@
 
 def main_kernel(
     dest_ref, shift_ref, ep_ref, x_ref, out_ref,
-    table, listed, koff_ref, held, zb, got, kof, place, sent, came, total, fall0, fall1, prod, split, acc, bands, result,
+    table, listed, koff_ref, held0, held, zb, got, kof, place, sent, came, total, fall0, fall1, prod, split, acc, bands, result,
     in_sem, own_sem, xs_sem, xr_sem, zs_sem, zr_sem, ys_sem, yr_sem, cs_sem, cr_sem, ks_sem, kr_sem, out_sem, table_sem,
 ):
     d = lax.axis_index("date")
@@ -67,7 +67,9 @@
     def load(q):
         half, date = divmod(q, 4)
         return pltpu.make_async_copy(
-            x_ref.at[:, :, date, :, pl.ds(half * 128, 128)], held.at[pl.ds(q * BLK, BLK)], in_sem.at[q]
+            x_ref.at[:, :, date, :, pl.ds(half * 128, 128)],
+            held0 if q == 0 else held.at[pl.ds((q - 1) * BLK, BLK)],
+            in_sem.at[q],
         )
 
     for q in range(NQ):
@@ -122,7 +124,7 @@
         )
 
     def way_of(q):
-        return 1 - 2 * lax.rem(q, 2)
+        return 1 - 2 * (q % 2 if isinstance(q, int) else lax.rem(q, 2))
 
     def koff_copies(par):
         copies = []
@@ -170,20 +172,19 @@
     for par in range(2):
         for copy in koff_copies(par):
             copy.start()
-    for q in range(NQ):
-        load(q).wait()
     table_copy.wait()
-
-    blocks = held.reshape(NQ * BLK, 2 * BR, 128)
-
-    def send_blocks(q):
-        par = lax.rem(q, 2)
+    load(0).wait()
+    blocks0 = held0.reshape(BLK, 2 * BR, 128)
+    blocks = held.reshape((NQ - 1) * BLK, 2 * BR, 128)
+
+    def send_blocks(q, source, first):
+        par = q % 2 if isinstance(q, int) else lax.rem(q, 2)
 
         @pl.loop(0, NT)
         def _(i):
             for k in range(CAP):
                 b = table[par * NT + i, k * 32]
-                v = blocks[q * BLK + jnp.minimum(jnp.maximum(b, 0), BLK - 1)]
+                v = source[first + jnp.minimum(jnp.maximum(b, 0), BLK - 1)]
                 zb[q, i, k * 32 : (k + 1) * 32, :] = jnp.where(b >= 0, v, jnp.zeros_like(v))
 
         for g in range(4):
@@ -205,9 +206,13 @@
                     hit = jnp.where(row == goal, 1.0, 0.0).astype(jnp.bfloat16)
                     place[par, j, i * 128 : (i + 1) * 128, s * 128 : (s + 1) * 128] = hit
 
-    @pl.loop(0, 3)
+    send_blocks(0, blocks0, 0)
+    for q in range(1, NQ):
+        load(q).wait()
+
+    @pl.loop(1, 3)
     def _(q):
-        send_blocks(q)
+        send_blocks(q, blocks, (q - 1) * BLK)
 
     build(0)
     build(1)
@@ -369,7 +374,7 @@
 
         @pl.when(step + 3 < NQ)
         def _():
-            send_blocks(step + 3)
+            send_blocks(step + 3, blocks, (step + 2) * BLK)
 
         for half, fall in enumerate((fall0, fall1)):
             first = half * 4
@@ -433,7 +438,8 @@
             pltpu.SMEM((2 * NT, 128), jnp.int32),
             pltpu.VMEM((2 * NT, 128), jnp.int32),
             pltpu.VMEM((2 * NT, 1, 128), jnp.int32),
-            pltpu.VMEM((NQ * BLK, BR, 2, 128), jnp.bfloat16),
+            pltpu.VMEM((BLK, BR, 2, 128), jnp.bfloat16),
+            pltpu.VMEM(((NQ - 1) * BLK, BR, 2, 128), jnp.bfloat16),
             pltpu.VMEM((NQ, NT, KS, 128), jnp.bfloat16),
             pltpu.VMEM((NQ, NZ, NX * KP, 128), jnp.bfloat16),
             pltpu.VMEM((2, NX, NZ, 1, 128), jnp.int32),

time: 128 us -> 128 us (level)
  no operation moved by 1% of the time
where the time goes in v7:
time: 128 us
  Pallas kernels  125 us (98%)
  local copies, waits for them, and re-layouts  3.05 us (2%)
    pallas_call x1, Pallas kernels, main_call(): pl.pallas_call(main_kernel, out_shape=jax.ShapeDtypeStruct((TR, NP, 256),...  125 us
    unnamed x1, local copies, waits for them, and re-layouts  3.05 us

profile of v7, /device:TPU:1, one launch (start us, length us, event | category | flops | bytes accessed | tf_op | source)
XLA Modules:
  0.0 127.9 jit_solution(10759998046644681842)
XLA Ops:
  0.0 124.8 %tiles_and_coherence.1 = f32[256,8,256]{2,1,0:T(8,128)} custom-call(s32[1,64]{1,0:T(1,128)} %bitcast.4, s32[1,64]{1,0:T(1,128)} %bitcast.5, s32[2,64]{1,0:T(2,128)} %bitcast.3, bf16[64,16,4,2,256]{4,3,2,1,0:T(2,128)(2,1)} %x_ref.1), custom_call_target="tpu_custom_call" | custom-call | tf_op jit(solution)/shard_map/tiles_and_coherence/pallas_call | solution.py:432
  124.9 3.0 %copy.6 = f32[256,8,256]{2,1,0:T(8,128)} copy(f32[256,8,256]{2,1,0:T(8,128)} %tiles_and_coherence.1) | data formatting | bytes 4194304
